TPU v7x, 256 devices: a whole 4x4x8 slice. The times are simulated.
256 devices in a mesh: node: 16 (over z_hi, y), slab: 16 (over x, z_lo, core).
Axes of the slice: x: 4, y: 4, z: 8 (z_hi: 4, z_lo: 2; z = z_hi * 2 + z_lo), core: 2. Of those that a mesh axis runs over, the one named last changes fastest.
Arguments:
- tensors: float32 [16, 128, 128, 128], P('node', 'slab'), may hold values from -0.375 to 0.375
- ops: float32 [8, 128, 128], replicated, as said below
- assign: int32 [16, 2], replicated, may hold values from 0 to 7
- parent: int32 [16], replicated, may hold values from 0 to 7, as said below
- env: float32 [128, 128], replicated, as said below
Outputs:
- gradient: float32 [16, 128, 128, 128], P('node', None, 'slab')
- energy: float32 [], replicated
Inputs may be any that keep to these rules, and one draw needn't show every extreme that they name: parent[0] = 0 and parent[1] = 0; for every level L from 2 to 4, each node of indices 2 ** (L - 1) to 2 ** L - 1 has its parent among indices 2 ** (L - 2) to 2 ** (L - 1) - 1, and each of those is the parent of exactly two of them. Every matrix ops[k] is symmetric. env is symmetric.
All inputs are finite; a program needn't handle non-finite values.
Results may differ from a plain program's by a relative error of at most 0.00012.
Values sent between devices are 32-bit elements; how exact they have to be, the bound alone decides.
A program may use at most 64 MiB of HBM per device.

v0:
```python
import jax
import jax.numpy as jnp
from jax import lax
from jax.sharding import PartitionSpec as P

LEVELS = 5
NODES = 16


HIGH = lax.Precision.HIGHEST


def links(parent):
    index = jnp.arange(NODES, dtype=jnp.int32)
    linked = (parent[None, :] == index[:, None]) & (index[None, :] >= 1)
    count = jnp.sum(linked.astype(jnp.int32), axis=1)
    left = jnp.min(jnp.where(linked, index[None, :], NODES), axis=1)
    right = jnp.max(jnp.where(linked, index[None, :], -1), axis=1)
    return (count, left, right)


def lookup(table, wanted):
    slots = jnp.arange(table.shape[0], dtype=jnp.int32)
    return jnp.sum(jnp.where(slots[None, :] == wanted[:, None], table[None, :], 0), axis=1)


def select_rows(onehot, stacked):
    return jnp.einsum("nm,mab->nab", onehot, stacked, precision=HIGH)


def per_device(tensors, ops, assign, parent, env):
    local_count = tensors.shape[0]
    width = tensors.shape[2]
    slab_rows = width // lax.axis_size("slab")
    node_ids = lax.axis_index("node") * local_count + jnp.arange(local_count, dtype=jnp.int32)
    slots = jnp.arange(NODES, dtype=jnp.int32)
    levels_all = jnp.zeros((NODES,), jnp.int32)
    for power in range(LEVELS - 1):
        levels_all = levels_all + (slots >= 2**power).astype(jnp.int32)
    my_level = lookup(levels_all, node_ids)
    count, left, right = links(parent)
    my_count = lookup(count, node_ids)
    my_left = lookup(left, node_ids)
    my_right = lookup(right, node_ids)
    table_ids = jnp.arange(ops.shape[0], dtype=jnp.int32)
    first_hot = (lookup(assign[:, 0], node_ids)[:, None] == table_ids[None, :]).astype(jnp.float32)
    second_hot = (lookup(assign[:, 1], node_ids)[:, None] == table_ids[None, :]).astype(jnp.float32)
    first_ops = jnp.einsum("nk,kab->nab", first_hot, ops, precision=HIGH)
    second_ops = jnp.einsum("nk,kab->nab", second_hot, ops, precision=HIGH)
    pair = jnp.einsum("nplr,nlm->npmr", tensors, first_ops, precision=HIGH)
    pair = jnp.einsum("npmr,nrs->npms", pair, second_ops, precision=HIGH)
    right_form = lax.all_to_all(
        tensors.transpose(0, 3, 1, 2), "slab", split_axis=1, concat_axis=2, tiled=True
    )
    left_form, pair_left = (
        lax.all_to_all(tensors, "slab", split_axis=2, concat_axis=1, tiled=True),
        lax.all_to_all(pair, "slab", split_axis=2, concat_axis=1, tiled=True),
    )
    zero_square = jnp.zeros((width, width), jnp.float32)
    left_store = jnp.zeros_like(right_form)
    right_store = jnp.zeros_like(left_form)
    left_ops = first_ops
    right_ops = second_ops
    onehot_left = (my_left[:, None] == slots[None, :]).astype(jnp.float32)
    onehot_right = (my_right[:, None] == slots[None, :]).astype(jnp.float32)
    energy = jnp.zeros((), jnp.float32)
    for level in range(LEVELS - 1, -1, -1):

        def climb(items, level=level):
            right_part, left_part, pair_part, left_op, right_op, left_old, right_old, node_level = (
                items
            )

            def climb_compute(unused):
                along_left = jnp.einsum("rpl,lm->rpm", right_part, left_op, precision=HIGH)
                along_right = (
                    jnp.einsum("plr,rs->pls", left_part, right_op, precision=HIGH) + pair_part
                )
                upper = jnp.einsum("rpm,rqm->pq", along_left, right_part, precision=HIGH)
                upper = upper + jnp.einsum("pls,qls->pq", along_right, left_part, precision=HIGH)
                return (along_left, along_right, upper)

            def climb_keep(unused):
                return (left_old, right_old, zero_square)

            return lax.cond(node_level == level, climb_compute, climb_keep, 0)

        left_store, right_store, partial_up = lax.map(
            climb,
            (
                right_form,
                left_form,
                pair_left,
                left_ops,
                right_ops,
                left_store,
                right_store,
                my_level,
            ),
        )
        up_rows = lax.psum_scatter(partial_up, "slab", scatter_dimension=1, tiled=True)
        if level > 0:
            every_rows = lax.all_gather(up_rows, "node", axis=0, tiled=True)
            left_rows = select_rows(onehot_left, every_rows)
            right_rows = select_rows(onehot_right, every_rows)
            left_full, right_full = (
                lax.all_gather(left_rows, "slab", axis=1, tiled=True),
                lax.all_gather(right_rows, "slab", axis=1, tiled=True),
            )
            ready = my_level == level - 1
            left_ops = jnp.where((ready & (my_count >= 1))[:, None, None], left_full, left_ops)
            right_ops = jnp.where((ready & (my_count >= 2))[:, None, None], right_full, right_ops)
        else:
            env_rows = lax.dynamic_slice_in_dim(
                env, lax.axis_index("slab") * slab_rows, slab_rows, 0
            )
            own = jnp.where(node_ids == 0, jnp.sum(up_rows * env_rows[None], axis=(1, 2)), 0.0)
            energy = lax.psum(jnp.sum(own), ("node", "slab"))
    down = jnp.where((node_ids == 0)[:, None, None], env[None], 0.0)
    parent_mine = lookup(parent, node_ids)
    is_left = lookup(left, parent_mine) == node_ids
    onehot_parent = (parent_mine[:, None] == slots[None, :]).astype(jnp.float32)
    for level in range(LEVELS - 1):

        def descend(items, level=level):
            right_part, left_part, down_now, node_level = items

            def descend_compute(unused):
                moved_r = jnp.einsum("pq,rql->rpl", down_now, right_part, precision=HIGH)
                down_left = jnp.einsum("rpl,rpm->lm", right_part, moved_r, precision=HIGH)
                moved_l = jnp.einsum("pq,qlr->plr", down_now, left_part, precision=HIGH)
                down_right = jnp.einsum("plr,pls->rs", left_part, moved_l, precision=HIGH)
                return (down_left, down_right)

            def descend_keep(unused):
                return (zero_square, zero_square)

            return lax.cond(node_level == level, descend_compute, descend_keep, 0)

        part_left, part_right = lax.map(descend, (right_form, left_form, down, my_level))
        rows_left, rows_right = (
            lax.psum_scatter(part_left, "slab", scatter_dimension=1, tiled=True),
            lax.psum_scatter(part_right, "slab", scatter_dimension=1, tiled=True),
        )
        every_left, every_right = (
            lax.all_gather(rows_left, "node", axis=0, tiled=True),
            lax.all_gather(rows_right, "node", axis=0, tiled=True),
        )
        from_left = select_rows(onehot_parent, every_left)
        from_right = select_rows(onehot_parent, every_right)
        mine = jnp.where(is_left[:, None, None], from_left, from_right)
        full_down = lax.all_gather(mine, "slab", axis=1, tiled=True)
        down = jnp.where((my_level == level + 1)[:, None, None], full_down, down)
    factor = width**0.75
    own_part = jnp.einsum("npq,nqlr->nplr", down, right_store, precision=HIGH)
    far_part = jnp.einsum("npq,nrql->nrpl", down, left_store, precision=HIGH)
    far_moved = lax.all_to_all(far_part, "slab", split_axis=3, concat_axis=1, tiled=True).transpose(
        0, 2, 3, 1
    )
    gradient = factor * (own_part + far_moved)
    return (gradient, energy)


def solution(mesh):
    return jax.shard_map(
        per_device,
        mesh=mesh,
        in_specs=(P("node", "slab", None, None), P(), P(), P(), P()),
        out_specs=(P("node", None, "slab", None), P()),
        check_vma=False,
    )
```

profile of v0, /device:TPU:1, one launch (start us, length us, event | category | flops | bytes accessed | tf_op | source)
XLA Modules:
  0.0 1453.6 jit_solution(2452833348320943357)
XLA Ops:
  8.6 1.4 fusion.39
  9.9 1.3 fusion.41
  13.5 7.2 all-to-all-start.2
  21.7 8.7 all-to-all-done.2
  30.4 4.6 all-to-all-start
  36.1 8.7 all-to-all-done
  44.8 4.8 all-to-all-start.1
  57.1 2.2 all-to-all-done.1
  59.3 1.7 conditional.13
  61.7 1.4 fusion.105
  63.1 3.3 conditional.9
  67.8 108.2 %all-reduce.23.cloned.1.call-done = f32[1,128,128]{2,1,0:T(8,128)} async-done(((f32[1,128,128]{2,1,0:T(8,128)}), f32[1,128,128]{2,1,0:T(8,128)}) %all-reduce.23.cloned.1.call-update) | async-done | bytes 65552
  176.7 37.1 %all_gather.84 = f32[16,8,128]{2,1,0:T(8,128)S(1)} all-gather(f32[1,8,128]{2,1,0:T(8,128)S(1)} %constant_dynamic-slice_fusion.3), channel_id=1, replica_groups=mesh['node'=16,'slab'=16] {'node'}, dimensions={0}, use_global_device_ids=true | all-gather | bytes 69632 | tf_op jit(solution)/shard_map/all_gather | solution.py:103
  215.3 25.6 %all-gather.5 = f32[128,128]{1,0:T(8,128)S(1)} all-gather(f32[8,128]{1,0:T(8,128)S(1)} %bitcast.485), channel_id=7, replica_groups=mesh['node'=16,'slab'=16] {'slab'}, dimensions={0}, use_global_device_ids=true | all-gather | bytes 69632 | tf_op jit(solution)/shard_map/all_gather | solution.py:108
  240.9 18.1 %all-gather.4 = f32[128,128]{1,0:T(8,128)S(1)} all-gather(f32[8,128]{1,0:T(8,128)S(1)} %bitcast.484), channel_id=6, replica_groups=mesh['node'=16,'slab'=16] {'slab'}, dimensions={0}, use_global_device_ids=true | all-gather | bytes 69632 | tf_op jit(solution)/shard_map/all_gather | solution.py:107
  263.6 106.7 %all-reduce.31.cloned.1.call-done = (f32[1,128,128]{2,1,0:T(8,128)}, f32[1,128,128]{2,0,1:T(1,128)}, f32[1,128,128]{2,0,1:T(1,128)}) async-done(((f32[1,128,128]{2,1,0:T(8,128)}, f32[1,128,128]{2,0,1:T(1,128)}, f32[1,128,128]{2,0,1:T(1,128)}), (f32[1,128,128]{2,1,0:T(8,128)}, f32[1,128,128]{2,0,1:T(1,128)}, f32[1,128,128]{2,0,1:T(1,128)})) %all-reduce.31.cloned.1.call-update) | async-done | bytes 196624
  370.9 37.4 %all_gather.87 = f32[16,8,128]{2,1,0:T(8,128)S(1)} all-gather(f32[1,8,128]{2,1,0:T(8,128)S(1)} %constant_dynamic-slice_fusion.2), channel_id=1, replica_groups=mesh['node'=16,'slab'=16] {'node'}, dimensions={0}, use_global_device_ids=true | all-gather | bytes 69632 | tf_op jit(solution)/shard_map/all_gather | solution.py:103
  411.3 24.4 %all-gather.7 = f32[128,128]{1,0:T(8,128)S(1)} all-gather(f32[8,128]{1,0:T(8,128)S(1)} %bitcast.477), channel_id=9, replica_groups=mesh['node'=16,'slab'=16] {'slab'}, dimensions={0}, use_global_device_ids=true | all-gather | bytes 69632 | tf_op jit(solution)/shard_map/all_gather | solution.py:108
  435.7 18.1 %all-gather.6 = f32[128,128]{1,0:T(8,128)S(1)} all-gather(f32[8,128]{1,0:T(8,128)S(1)} %bitcast.475), channel_id=8, replica_groups=mesh['node'=16,'slab'=16] {'slab'}, dimensions={0}, use_global_device_ids=true | all-gather | bytes 69632 | tf_op jit(solution)/shard_map/all_gather | solution.py:107
  453.8 31.3 %all_gather.73 = f32[16,8,128]{2,1,0:T(8,128)S(1)} all-gather(f32[1,8,128]{2,1,0:T(8,128)S(1)} %bitcast.492), channel_id=1, replica_groups=mesh['node'=16,'slab'=16] {'node'}, dimensions={0}, use_global_device_ids=true | all-gather | bytes 69632 | tf_op jit(solution)/shard_map/all_gather | solution.py:147
  485.9 33.3 %all_gather.72 = f32[16,8,128]{2,1,0:T(8,128)S(1)} all-gather(f32[1,8,128]{2,1,0:T(8,128)S(1)} %bitcast.489), channel_id=1, replica_groups=mesh['node'=16,'slab'=16] {'node'}, dimensions={0}, use_global_device_ids=true | all-gather | bytes 69632 | tf_op jit(solution)/shard_map/all_gather | solution.py:146
  520.0 30.2 %all-gather = f32[128,128]{1,0:T(8,128)S(1)} all-gather(f32[8,128]{1,0:T(8,128)S(1)} %broadcast_select_fusion.4), channel_id=2, replica_groups=mesh['node'=16,'slab'=16] {'slab'}, dimensions={0}, use_global_device_ids=true | all-gather | bytes 69632 | tf_op jit(solution)/shard_map/all_gather | solution.py:152
  552.5 112.1 %all-reduce.29.cloned.1.call-done = (f32[1,128,128]{2,1,0:T(8,128)}, f32[1,128,128]{2,0,1:T(1,128)}, f32[1,128,128]{2,0,1:T(1,128)}) async-done(((f32[1,128,128]{2,1,0:T(8,128)}, f32[1,128,128]{2,0,1:T(1,128)}, f32[1,128,128]{2,0,1:T(1,128)}), (f32[1,128,128]{2,1,0:T(8,128)}, f32[1,128,128]{2,0,1:T(1,128)}, f32[1,128,128]{2,0,1:T(1,128)})) %all-reduce.29.cloned.1.call-update) | async-done | bytes 196624
  665.3 37.4 %all_gather.90 = f32[16,8,128]{2,1,0:T(8,128)S(1)} all-gather(f32[1,8,128]{2,1,0:T(8,128)S(1)} %constant_dynamic-slice_fusion.1), channel_id=1, replica_groups=mesh['node'=16,'slab'=16] {'node'}, dimensions={0}, use_global_device_ids=true | all-gather | bytes 69632 | tf_op jit(solution)/shard_map/all_gather | solution.py:103
  705.7 24.4 %all-gather.9 = f32[128,128]{1,0:T(8,128)S(1)} all-gather(f32[8,128]{1,0:T(8,128)S(1)} %bitcast.478), channel_id=11, replica_groups=mesh['node'=16,'slab'=16] {'slab'}, dimensions={0}, use_global_device_ids=true | all-gather | bytes 69632 | tf_op jit(solution)/shard_map/all_gather | solution.py:108
  730.0 18.1 %all-gather.8 = f32[128,128]{1,0:T(8,128)S(1)} all-gather(f32[8,128]{1,0:T(8,128)S(1)} %bitcast.476), channel_id=10, replica_groups=mesh['node'=16,'slab'=16] {'slab'}, dimensions={0}, use_global_device_ids=true | all-gather | bytes 69632 | tf_op jit(solution)/shard_map/all_gather | solution.py:107
  748.2 31.3 %all_gather.76 = f32[16,8,128]{2,1,0:T(8,128)S(1)} all-gather(f32[1,8,128]{2,1,0:T(8,128)S(1)} %bitcast.493), channel_id=1, replica_groups=mesh['node'=16,'slab'=16] {'node'}, dimensions={0}, use_global_device_ids=true | all-gather | bytes 69632 | tf_op jit(solution)/shard_map/all_gather | solution.py:147
  780.3 33.3 %all_gather.75 = f32[16,8,128]{2,1,0:T(8,128)S(1)} all-gather(f32[1,8,128]{2,1,0:T(8,128)S(1)} %bitcast.490), channel_id=1, replica_groups=mesh['node'=16,'slab'=16] {'node'}, dimensions={0}, use_global_device_ids=true | all-gather | bytes 69632 | tf_op jit(solution)/shard_map/all_gather | solution.py:146
  814.4 30.2 %all-gather.1 = f32[128,128]{1,0:T(8,128)S(1)} all-gather(f32[8,128]{1,0:T(8,128)S(1)} %broadcast_select_fusion.3), channel_id=3, replica_groups=mesh['node'=16,'slab'=16] {'slab'}, dimensions={0}, use_global_device_ids=true | all-gather | bytes 69632 | tf_op jit(solution)/shard_map/all_gather | solution.py:152
  847.0 113.2 %all-reduce.27.cloned.1.call-done = (f32[1,128,128]{2,1,0:T(8,128)}, f32[1,128,128]{2,0,1:T(1,128)}, f32[1,128,128]{2,0,1:T(1,128)}) async-done(((f32[1,128,128]{2,1,0:T(8,128)}, f32[1,128,128]{2,0,1:T(1,128)}, f32[1,128,128]{2,0,1:T(1,128)}), (f32[1,128,128]{2,1,0:T(8,128)}, f32[1,128,128]{2,0,1:T(1,128)}, f32[1,128,128]{2,0,1:T(1,128)})) %all-reduce.27.cloned.1.call-update) | async-done | bytes 196624
  960.9 37.4 %all_gather.93 = f32[16,8,128]{2,1,0:T(8,128)S(1)} all-gather(f32[1,8,128]{2,1,0:T(8,128)S(1)} %constant_dynamic-slice_fusion), channel_id=1, replica_groups=mesh['node'=16,'slab'=16] {'node'}, dimensions={0}, use_global_device_ids=true | all-gather | bytes 69632 | tf_op jit(solution)/shard_map/all_gather | solution.py:103
  1001.2 24.3 %all-gather.11 = f32[128,128]{1,0:T(8,128)S(1)} all-gather(f32[8,128]{1,0:T(8,128)S(1)} %bitcast.473), channel_id=13, replica_groups=mesh['node'=16,'slab'=16] {'slab'}, dimensions={0}, use_global_device_ids=true | all-gather | bytes 69632 | tf_op jit(solution)/shard_map/all_gather | solution.py:108
  1025.6 18.1 %all-gather.10 = f32[128,128]{1,0:T(8,128)S(1)} all-gather(f32[8,128]{1,0:T(8,128)S(1)} %bitcast.474), channel_id=12, replica_groups=mesh['node'=16,'slab'=16] {'slab'}, dimensions={0}, use_global_device_ids=true | all-gather | bytes 69632 | tf_op jit(solution)/shard_map/all_gather | solution.py:107
  1043.7 31.3 %all_gather.79 = f32[16,8,128]{2,1,0:T(8,128)S(1)} all-gather(f32[1,8,128]{2,1,0:T(8,128)S(1)} %bitcast.494), channel_id=1, replica_groups=mesh['node'=16,'slab'=16] {'node'}, dimensions={0}, use_global_device_ids=true | all-gather | bytes 69632 | tf_op jit(solution)/shard_map/all_gather | solution.py:147
  1075.8 33.3 %all_gather.78 = f32[16,8,128]{2,1,0:T(8,128)S(1)} all-gather(f32[1,8,128]{2,1,0:T(8,128)S(1)} %bitcast.491), channel_id=1, replica_groups=mesh['node'=16,'slab'=16] {'node'}, dimensions={0}, use_global_device_ids=true | all-gather | bytes 69632 | tf_op jit(solution)/shard_map/all_gather | solution.py:146
  1109.9 30.2 %all-gather.2 = f32[128,128]{1,0:T(8,128)S(1)} all-gather(f32[8,128]{1,0:T(8,128)S(1)} %broadcast_select_fusion.2), channel_id=4, replica_groups=mesh['node'=16,'slab'=16] {'slab'}, dimensions={0}, use_global_device_ids=true | all-gather | bytes 69632 | tf_op jit(solution)/shard_map/all_gather | solution.py:152
  1141.6 6.6 conditional.17
  1144.7 1.4 convolution_bitcast_fusion.21
  1146.1 2.1 fusion.29
  1149.5 108.8 %all-reduce.25.cloned.1.call-done = (f32[1,128,128]{2,0,1:T(1,128)}, f32[1,128,128]{2,0,1:T(1,128)}, f32[1,128,128]{2,1,0:T(8,128)}) async-done(((f32[1,128,128]{2,0,1:T(1,128)}, f32[1,128,128]{2,0,1:T(1,128)}, f32[1,128,128]{2,1,0:T(8,128)}), (f32[1,128,128]{2,0,1:T(1,128)}, f32[1,128,128]{2,0,1:T(1,128)}, f32[1,128,128]{2,1,0:T(8,128)})) %all-reduce.25.cloned.1.call-update) | async-done | bytes 196624
  1259.6 37.4 %all_gather.81 = f32[16,8,128]{2,1,0:T(8,128)S(1)} all-gather(f32[1,8,128]{2,1,0:T(8,128)S(1)} %bitcast.496), channel_id=1, replica_groups=mesh['node'=16,'slab'=16] {'node'}, dimensions={0}, use_global_device_ids=true | all-gather | bytes 69632 | tf_op jit(solution)/shard_map/all_gather | solution.py:146
  1297.8 31.3 %all_gather.82 = f32[16,8,128]{2,1,0:T(8,128)S(1)} all-gather(f32[1,8,128]{2,1,0:T(8,128)S(1)} %bitcast.495), channel_id=1, replica_groups=mesh['node'=16,'slab'=16] {'node'}, dimensions={0}, use_global_device_ids=true | all-gather | bytes 69632 | tf_op jit(solution)/shard_map/all_gather | solution.py:147
  1329.9 31.3 %all-gather.3 = f32[128,128]{1,0:T(8,128)S(1)} all-gather(f32[8,128]{1,0:T(8,128)S(1)} %broadcast_select_fusion.1), channel_id=5, replica_groups=mesh['node'=16,'slab'=16] {'slab'}, dimensions={0}, use_global_device_ids=true | all-gather | bytes 69632 | tf_op jit(solution)/shard_map/all_gather | solution.py:152
  1361.2 1.6 convolution_bitcast_fusion.24
  1362.9 1.1 copy.233
  1364.0 3.5 all-to-all-start.3
  1367.5 1.3 fusion.78
  1369.4 75.3 %psum.7 = f32[]{:T(128)} all-reduce(f32[]{:T(128)S(6)} %select_n.174), channel_id=1, replica_groups=mesh['node'=16,'slab'=16] {'node','slab'}, use_global_device_ids=true, to_apply=%region_43.44 | all-reduce | flops 1 | bytes 8 | tf_op jit(solution)/shard_map/psum | solution.py:118
  (139 shorter events, 49.0 us)
Async XLA Ops:
  7.2 1.4 copy-start
  7.2 0.7 copy-start.15
  8.6 2.7 copy-start.6
  13.5 16.8 %all-to-all-start.2 = ((f32[1,8,128,128]{3,1,0,2:T(8,128)}), f32[1,8,128,128]{3,1,0,2:T(8,128)S(1)}, u32[]{:S(2)}, u32[]{:S(2)}) async-start(f32[1,8,128,128]{3,1,0,2:T(8,128)} %copy.218), calls=%async_computation.2 | async-start | bytes 1048576 | tf_op jit(solution)/shard_map/all_to_all | solution.py:57
  30.4 14.4 all-to-all-start
  44.7 7.4 copy-start.16
  44.7 10.2 copy-start.17
  44.8 14.5 all-to-all-start.1
  49.5 7.3 copy-start.9
  49.5 126.5 %all-reduce.23.cloned.1.call-start = ((), (), s32[]{:S(2)}) async-start(), calls=%async_computation.4 | async-start | bytes 131072
  61.0 0.6 copy-start.14
  61.7 308.6 %all-reduce.31.cloned.1.call-start = ((), (), s32[]{:S(2)}) async-start(), calls=%async_computation.8 | async-start | bytes 393216
  259.6 0.6 copy-start.11
  260.3 404.3 %all-reduce.29.cloned.1.call-start = ((), (), s32[]{:S(2)}) async-start(), calls=%async_computation.7 | async-start | bytes 393216
  551.8 0.6 copy-start.12
  552.4 407.7 %all-reduce.27.cloned.1.call-start = ((), (), s32[]{:S(2)}) async-start(), calls=%async_computation.6 | async-start | bytes 393216
  846.3 0.6 copy-start.13
  847.0 411.3 %all-reduce.25.cloned.1.call-start = ((), (), s32[]{:S(2)}) async-start(), calls=%async_computation.5 | async-start | bytes 393216
  1140.1 1.5 copy-start.5
  1143.5 1.0 copy-start.7
  1146.1 2.1 copy-start.8
  1148.2 0.6 copy-start.10
  1364.0 80.8 %all-to-all-start.3 = ((f32[1,8,128,128]{2,1,0,3:T(8,128)}), f32[1,8,128,128]{2,1,0,3:T(8,128)S(1)}, u32[]{:S(2)}, u32[]{:S(2)}) async-start(f32[1,8,128,128]{2,1,0,3:T(8,128)} %copy.233), calls=%async_computation.3 | async-start | bytes 1048576 | tf_op jit(solution)/shard_map/all_to_all | solution.py:157
Sparse Core Ops, SparseCore 0:
  61.8 114.1 all-reduce.22
  260.4 109.8 all-reduce.30
  552.6 111.9 all-reduce.28
  847.1 113.0 all-reduce.26
  1149.0 109.2 all-reduce.24
where the time goes:
time: 1460 us; the launch traced here: 1450 us
  blocking collectives  780 us (53%)
  waiting for transfers between devices  569 us (39%)
  matrix products  27.1 us (2%)
  local copies, waits for them, and re-layouts  26.8 us (2%)
  between operations  23.6 us (2%)
  starting transfers between devices  20.3 us (1%)
    unnamed x10, waiting for transfers between devices  549 us
    all_gather x4, blocking collectives, per_device(): every_rows = lax.all_gather(up_rows, 'node', axis=0, tiled=True)  149 us
    all_gather x4, blocking collectives, per_device(): lax.all_gather(rows_left, 'node', axis=0, tiled=True)  137 us
    all_gather x4, blocking collectives, per_device(): lax.all_gather(rows_right, 'node', axis=0, tiled=True)  125 us
    all_gather x4, blocking collectives, per_device(): full_down = lax.all_gather(mine, 'slab', axis=1, tiled=True)  122 us
    all_gather x4, blocking collectives, per_device(): lax.all_gather(right_rows, 'slab', axis=1, tiled=True)  98.7 us
    psum x1, blocking collectives, per_device(): energy = lax.psum(jnp.sum(own), ('node', 'slab'))  75.3 us
    all_gather x4, blocking collectives, per_device(): lax.all_gather(left_rows, 'slab', axis=1, tiled=True)  72.6 us
  transfers between devices with their start and end apart: 9, of which 8 were waited for; matrix products, arithmetic and copies ran while one was open for 1% of the time, Pallas kernels for 0%

commit v1 on v0

v1 whole, which is shorter than its diff:
```python
import functools

import jax
import jax.numpy as jnp
from jax import lax
from jax.experimental import pallas as pl
from jax.experimental.pallas import tpu as pltpu
from jax.sharding import PartitionSpec as P

NODES = 16
MESH = pl.DeviceIdType.MESH
F32 = jnp.float32
BF16 = jnp.bfloat16

A2A_R, A2A_L, A2A_K, A2A_X, RS_U, RS_D, AG_U, AG_D, SLAB_E, NODE_U, NODE_D, NODE_E = range(12)


def split(x):
    hi = x.astype(BF16)
    return hi, (x - hi.astype(F32)).astype(BF16)


def dot(a, b, nt):
    dims = (((1,), (1 if nt else 0,)), ((), ()))
    return lax.dot_general(a, b, dims, preferred_element_type=F32)


def mm(a, b, nt=False):
    return dot(a[0], b[0], nt) + (dot(a[0], b[1], nt) + dot(a[1], b[0], nt))


def kernel(
    ns, t_ref, ops_ref, env_ref, assign_ref, parent_ref, out_ref, en_ref,
    flat, s_r, s_l, s_k, s_x, t_r, t_l, k_l, x_l,
    th, tl, lh, ll, rh, rl, lth, ltl, rth, rtl,
    up, rs_u, u_row, u_cand, xy_row, xy,
    dp, rs_d, d_row, d_cand, dd_row, dd,
    rs_e, e_row, e_cand, ss, rs,
):
    n = lax.axis_index("node")
    s = lax.axis_index("slab")
    b = env_ref.shape[0]
    w = b // ns
    rows = pl.ds(pl.multiple_of(s * w, w), w)
    leaf = n >= 8

    def block(j):
        return pl.ds(pl.multiple_of(j * w, w), w)

    c0 = jnp.where(n >= 4, 8, jnp.where(n >= 2, 4, jnp.where(n >= 1, 2, 1)))
    c1 = jnp.where(n >= 1, 2 * c0, 2)
    p0 = jnp.where(n >= 8, 4, jnp.where(n >= 4, 2, jnp.where(n >= 2, 1, 0)))
    p1 = jnp.where(n >= 2, 2 * p0, 1)

    barrier = pltpu.get_barrier_semaphore()

    def greet_slab(k, c):
        pl.semaphore_signal(barrier, inc=1, device_id=(n, lax.rem(s + k, ns)), device_id_type=MESH)
        return c

    def greet_node(k, c):
        pl.semaphore_signal(barrier, inc=1, device_id=(lax.rem(n + k, NODES), s), device_id_type=MESH)
        return c

    lax.fori_loop(1, ns, greet_slab, 0)
    lax.fori_loop(1, NODES, greet_node, 0)

    def slab_copy(q, src, dst, to, frm):
        return pltpu.make_async_remote_copy(
            src_ref=src, dst_ref=dst, send_sem=ss.at[q, to], recv_sem=rs.at[q, frm],
            device_id=(n, to), device_id_type=MESH,
        )

    def slab_start(q, src_of, dst):
        def go(k, c):
            j = lax.rem(s + k, ns)
            slab_copy(q, src_of(j), dst, j, s).start()
            return c

        lax.fori_loop(1, ns, go, 0)

    def slab_wait(q, dst_of):
        def go(k, c):
            i = lax.rem(s + k, ns)
            slab_copy(q, dst_of(i), dst_of(i), i, i).wait_recv()
            return c

        lax.fori_loop(1, ns, go, 0)

    def slab_drain(q, src_of):
        def go(k, c):
            j = lax.rem(s + k, ns)
            slab_copy(q, src_of(j), src_of(j), j, s).wait_send()
            return c

        lax.fori_loop(1, ns, go, 0)

    def node_copy(q, src, dst, to, frm):
        return pltpu.make_async_remote_copy(
            src_ref=src, dst_ref=dst, send_sem=ss.at[q, to], recv_sem=rs.at[q, frm],
            device_id=(to, s), device_id_type=MESH,
        )

    def node_start(q, src, dst, lo, hi):
        def go(m, c):
            node_copy(q, src, dst, m, n).start()
            return c

        lax.fori_loop(lo, hi, go, 0)

    def node_wait(q, dst_of, lo, hi):
        def go(m, c):
            node_copy(q, dst_of(m), dst_of(m), m, m).wait_recv()
            return c

        lax.fori_loop(lo, hi, go, 0)

    def node_drain(q, src, lo, hi):
        def go(m, c):
            node_copy(q, src, src, m, n).wait_send()
            return c

        lax.fori_loop(lo, hi, go, 0)

    def relayout(src, dst):
        for i in range(b):
            dst[i] = src[pl.ds(i, w, stride=b), :]

    def a2a_start(q, src, dst):
        slab_start(q, lambda j: src.at[block(j)], dst.at[:, rows, :])
        dst[:, rows, :] = src[rows]

    def a2a_wait(q, dst):
        slab_wait(q, lambda i: dst.at[:, block(i), :])

    def a2a_drain(q, src):
        slab_drain(q, lambda j: src.at[block(j)])

    def both(h, l, i):
        return h[i * b : (i + 1) * b, :], l[i * b : (i + 1) * b, :]

    def sandwich(h, l, x, add=None):
        total = jnp.zeros((b, b), F32)
        for i in range(w):
            m = both(h, l, i)
            moved = mm(m, x)
            if add is not None:
                add[i] = add[i] + moved
            total = total + mm(split(moved), m, nt=True)
        return total

    def store_split(h, l, i, x):
        h[i * b : (i + 1) * b, :], l[i * b : (i + 1) * b, :] = split(x)

    op_p = split(ops_ref[assign_ref[n, 0]])
    op_q = split(ops_ref[assign_ref[n, 1]])

    @pl.when(n < 8)
    def _():
        for i in range(w):
            flat[i * b : (i + 1) * b, :] = t_ref[i * b : (i + 1) * b, :].T
        relayout(flat, s_r)

    relayout(t_ref, s_l)
    pl.semaphore_wait(barrier, ns - 1 + NODES - 1)

    @pl.when(n < 8)
    def _():
        a2a_start(A2A_R, s_r, t_r)

    a2a_start(A2A_L, s_l, t_l)
    for i in range(w):
        store_split(th, tl, i, t_ref[i * b : (i + 1) * b, :])
    for i in range(w):
        t = t_ref[i * b : (i + 1) * b, :]
        tq = mm(both(th, tl, i), op_q)
        v = jnp.where(leaf, t + tq, tq)
        flat[i * b : (i + 1) * b, :] = mm(op_p, split(v)) + jnp.where(leaf, tq, 0.0)
    relayout(flat, s_k)
    a2a_start(A2A_K, s_k, k_l)

    @pl.when(n < 8)
    def _():
        a2a_wait(A2A_R, t_r)
        for i in range(w):
            store_split(rth, rtl, i, t_r[i].T)
            store_split(rh, rl, i, t_r[i])

    a2a_wait(A2A_L, t_l)
    for i in range(w):
        store_split(lh, ll, i, t_l[i])

    @pl.when(n < 8)
    def _():
        for i in range(w):
            store_split(lth, ltl, i, t_l[i].T)

    def pair_square():
        a2a_wait(A2A_K, k_l)
        total = jnp.zeros((b, b), F32)
        for i in range(w):
            total = total + mm(split(k_l[i]), both(lh, ll, i), nt=True)
        up[...] = total

    def family(m):
        first = jnp.int32(NODES)
        last = jnp.int32(0)
        for k in range(NODES - 1, 0, -1):
            hit = parent_ref[k] == m
            first = jnp.where(hit, k, first)
        for k in range(1, NODES):
            last = jnp.where(parent_ref[k] == m, k, last)
        return jnp.minimum(first, NODES - 1), last

    def receive_d():
        node_wait(NODE_D, lambda m: d_cand.at[m], p0, p1)
        mine = parent_ref[n]
        first, _ = family(mine)
        side = jnp.where(first == n, 0, 1)
        dd_row[...] = d_cand[mine, side]
        slab_start(AG_D, lambda j: dd_row, dd.at[rows, :])
        dd[rows, :] = dd_row[...]
        slab_wait(AG_D, lambda i: dd.at[block(i), :])

    def send_d():
        d = split(dd[...])
        dp[0] = sandwich(rth, rtl, d)
        dp[1] = sandwich(lth, ltl, d)
        slab_start(RS_D, lambda j: dp.at[:, block(j), :], rs_d.at[s])
        rs_d[s] = dp[:, rows, :]
        slab_wait(RS_D, lambda i: rs_d.at[i])
        total = rs_d[0]
        for k in range(1, ns):
            total = total + rs_d[k]
        d_row[...] = total
        node_start(NODE_D, d_row, d_cand.at[n], c0, c1)

    def send_u():
        slab_start(RS_U, lambda j: up.at[block(j), :], rs_u.at[s])
        rs_u[s] = up[rows, :]
        slab_wait(RS_U, lambda i: rs_u.at[i])
        total = rs_u[0]
        for k in range(1, ns):
            total = total + rs_u[k]
        u_row[...] = total
        node_start(NODE_U, u_row, u_cand.at[n], p0, p1)

    def receive_u():
        first, last = family(n)
        node_wait(NODE_U, lambda m: u_cand.at[m], c0, c1)
        xy_row[0] = u_cand[first]
        second = u_cand[last]
        xy_row[1] = jnp.where(n == 0, ops_ref[assign_ref[n, 1], rows, :], second)
        slab_start(AG_U, lambda j: xy_row, xy.at[:, rows, :])
        xy[:, rows, :] = xy_row[...]
        slab_wait(AG_U, lambda i: xy.at[:, block(i), :])

    def move_left(x):
        for i in range(w):
            flat[i * b : (i + 1) * b, :] = mm(x, both(th, tl, i))
        relayout(flat, s_x)
        a2a_start(A2A_X, s_x, x_l)

    def send_energy(square):
        terms = dd[...] * square
        total = terms[0:w, :]
        for k in range(1, ns):
            total = total + terms[k * w : (k + 1) * w, :]
        rs_e[s] = total
        slab_start(SLAB_E, lambda j: rs_e.at[s], rs_e.at[s])

    def share_energy():
        slab_wait(SLAB_E, lambda i: rs_e.at[i])
        total = rs_e[0]
        for k in range(1, ns):
            total = total + rs_e[k]
        e_cand[n] = total

        def go(k, c):
            m = lax.rem(n + k, NODES)
            node_copy(NODE_E, e_cand.at[n], e_cand.at[n], m, n).start()
            return c

        lax.fori_loop(1, NODES, go, 0)

    def climb():
        receive_u()
        x = split(xy[0])
        y = split(xy[1])
        up[...] = up[...] + sandwich(rh, rl, x) + sandwich(lh, ll, y, add=k_l)
        send_u()
        move_left(x)

    @pl.when(leaf)
    def _():
        pair_square()
        send_u()
        receive_d()

    @pl.when((n >= 4) & (n < 8))
    def _():
        pair_square()
        climb()
        receive_d()
        send_d()

    @pl.when((n >= 1) & (n < 4))
    def _():
        receive_d()
        send_d()
        pair_square()

        @pl.when(n == 1)
        def _():
            send_energy(up[...])
            share_energy()

        climb()

        @pl.when(n > 1)
        def _():
            send_energy(up[...])
            share_energy()

    @pl.when(n == 0)
    def _():
        dd[...] = env_ref[...]
        send_d()
        pair_square()
        send_energy(up[...] + sandwich(lh, ll, op_q, add=k_l))
        share_energy()
        receive_u()
        move_left(split(xy[0]))

    factor = b**0.75
    d = split(dd[...])

    @pl.when(n < 8)
    def _():
        a2a_wait(A2A_X, x_l)

    for i in range(w):
        part = k_l[i] + jnp.where(n < 8, x_l[i], 0.0)
        out_ref[i] = factor * mm(d, split(part))

    def energy_wait(m, c):
        @pl.when(m != n)
        def _():
            node_copy(NODE_E, e_cand.at[m], e_cand.at[m], m, m).wait_recv()

        return c

    lax.fori_loop(0, 4, energy_wait, 0)
    total = (e_cand[0] + e_cand[1]) + (e_cand[2] + e_cand[3])
    en_ref[...] = jnp.sum(total, axis=(0, 1), keepdims=True)

    a2a_drain(A2A_L, s_l)
    a2a_drain(A2A_K, s_k)

    @pl.when(n < 8)
    def _():
        a2a_drain(A2A_R, s_r)
        a2a_drain(A2A_X, s_x)
        slab_drain(RS_D, lambda j: dp.at[:, block(j), :])
        node_drain(NODE_D, d_row, c0, c1)
        slab_drain(AG_U, lambda j: xy_row)

    @pl.when(n >= 1)
    def _():
        slab_drain(RS_U, lambda j: up.at[block(j), :])
        node_drain(NODE_U, u_row, p0, p1)
        slab_drain(AG_D, lambda j: dd_row)

    @pl.when(n < 4)
    def _():
        slab_drain(SLAB_E, lambda j: rs_e.at[s])

        def go(k, c):
            m = lax.rem(n + k, NODES)
            node_copy(NODE_E, e_cand.at[n], e_cand.at[n], m, n).wait_send()
            return c

        lax.fori_loop(1, NODES, go, 0)


def per_device(ns, tensors, ops, assign, parent, env):
    b = env.shape[0]
    w = b // ns
    full = pltpu.VMEM((b, w, b), F32)
    form = pltpu.VMEM((w, b, b), F32)
    half = pltpu.VMEM((w * b, b), BF16)
    square = pltpu.VMEM((b, b), F32)
    slots = max(ns, NODES)
    vmem = pl.BlockSpec(memory_space=pltpu.VMEM)
    smem = pl.BlockSpec(memory_space=pltpu.SMEM)
    grad, energy = pl.pallas_call(
        functools.partial(kernel, ns),
        out_shape=(jax.ShapeDtypeStruct((w, b, b), F32), jax.ShapeDtypeStruct((1, 1), F32)),
        in_specs=[vmem, vmem, vmem, smem, smem],
        out_specs=(vmem, vmem),
        scratch_shapes=[
            pltpu.VMEM((w * b, b), F32), full, full, full, full, form, form, form, form,
            half, half, half, half, half, half, half, half, half, half,
            square, pltpu.VMEM((ns, w, b), F32), pltpu.VMEM((w, b), F32),
            pltpu.VMEM((NODES, w, b), F32), pltpu.VMEM((2, w, b), F32), pltpu.VMEM((2, b, b), F32),
            pltpu.VMEM((2, b, b), F32), pltpu.VMEM((ns, 2, w, b), F32), pltpu.VMEM((2, w, b), F32),
            pltpu.VMEM((NODES, 2, w, b), F32), pltpu.VMEM((w, b), F32), square,
            pltpu.VMEM((ns, w, b), F32), pltpu.VMEM((w, b), F32), pltpu.VMEM((NODES, w, b), F32),
            pltpu.SemaphoreType.DMA((12, slots)), pltpu.SemaphoreType.DMA((12, slots)),
        ],
        compiler_params=pltpu.CompilerParams(collective_id=0, has_side_effects=True),
    )(tensors.reshape(w * b, b), ops, env, assign, parent)
    return grad.transpose(1, 0, 2)[None], energy[0, 0]


def solution(mesh):
    return jax.shard_map(
        functools.partial(per_device, mesh.shape["slab"]),
        mesh=mesh,
        in_specs=(P("node", "slab", None, None), P(), P(), P(), P()),
        out_specs=(P("node", None, "slab", None), P()),
        check_vma=False,
    )
```

time: 1460 us -> 115 us (0.08)
  blocking collectives: 780 us -> 0 us
  waiting for transfers between devices: 569 us -> 0 us
  Pallas kernels: 0 us -> 108 us
  matrix products: 27.1 us -> 0 us
  local copies, waits for them, and re-layouts: 26.8 us -> 3.49 us
  between operations: 23.6 us -> 2.41 us
  starting transfers between devices: 20.3 us -> 0 us
    all_gather x24 -> x0, blocking collectives: 705 us -> none  [the longest x4 149 us: per_device(): every_rows = lax.all_gather(up_rows, 'node', axis=0, tiled=True)]
    unnamed x10 -> x0, waiting for transfers between devices: 549 us -> none
    pallas_call x0 -> x1, Pallas kernels: none -> 108 us  [per_device(): pl.pallas_call(functools.partial(kernel, ns), out_shape=(jax.ShapeDtypeSt...]
    psum x1 -> x0, blocking collectives: 75.3 us -> none  [per_device(): energy = lax.psum(jnp.sum(own), ('node', 'slab'))]
    dot_general x30 -> x0, matrix products: 27.1 us -> none  [the longest x16 12.7 us: select_rows(): return jnp.einsum('nm,mab->nab', onehot, stacked, precision=HIGH)]
    all_to_all x4 -> x0, starting transfers between devices: 20.1 us -> none  [the longest x1 7.16 us: per_device(): lax.all_to_all(pair, 'slab', split_axis=2, concat_axis=1, tiled=True)]
    all_to_all x4 -> x0, waiting for transfers between devices: 19.5 us -> none  [the longest x1 8.67 us: per_device(): lax.all_to_all(pair, 'slab', split_axis=2, concat_axis=1, tiled=True)]
  transfers between devices with their start and end apart: 9 -> 0, of which waited for: 8 -> 0; matrix products, arithmetic and copies ran while one was open for 1% -> 0% of each run, Pallas kernels for 0% -> 0%
where the time goes in v1:
time: 115 us; the launch traced here: 114 us
  Pallas kernels  108 us (94%)
  local copies, waits for them, and re-layouts  3.49 us (3%)
  between operations  2.41 us (2%)
    pallas_call x1, Pallas kernels, per_device(): pl.pallas_call(functools.partial(kernel, ns), out_shape=(jax.ShapeDtypeSt...  108 us
    unnamed x4, local copies, waits for them, and re-layouts  3.49 us

profile of v1, /device:TPU:1, one launch (start us, length us, event | category | flops | bytes accessed | tf_op | source)
XLA Modules:
  0.0 114.4 jit_solution(11830234781401229979)
XLA Ops:
  0.6 0.0 copy-start
  0.6 0.7 copy-done
  1.3 0.7 copy.7.assign_ref
  2.0 108.4 %shard_map.68 = (f32[8,128,128]{2,1,0:T(8,128)}, f32[1,1]{1,0:T(1,128)}) custom-call(f32[1024,128]{1,0:T(8,128)} %bitcast.5, f32[8,128,128]{2,1,0:T(8,128)} %ops_ref.1, f32[128,128]{1,0:T(8,128)} %env_ref.1, s32[16,2]{1,0:T(8,128)} %copy.7.assign_ref, s32[16]{0:T(128)} %parent_ref.1), custom_call_target="tpu_custom_call" | custom-call | tf_op jit(solution)/shard_map/pallas_call | solution.py:396
  110.4 2.1 %copy.8 = f32[1,128,8,128]{3,2,1,0:T(8,128)} copy(f32[1,128,8,128]{3,1,2,0:T(8,128)} %bitcast.6) | data formatting | bytes 1048576
Async XLA Ops:
  0.6 0.7 copy-start

commit v2 on v1

v2 whole, which is shorter than its diff:
```python
import functools

import jax
import jax.numpy as jnp
from jax import lax
from jax.experimental import pallas as pl
from jax.experimental.pallas import tpu as pltpu
from jax.sharding import PartitionSpec as P

NODES = 16
MESH = pl.DeviceIdType.MESH
F32 = jnp.float32
BF16 = jnp.bfloat16

A2A_R, A2A_L, A2A_K, A2A_X, RS_U, RS_D, AG_U, AG_D, SLAB_E, NODE_U, NODE_D, NODE_E, NODE_F = range(13)


def split(x):
    hi = x.astype(BF16)
    return hi, (x - hi.astype(F32)).astype(BF16)


def beside(x):
    return jnp.concatenate(split(x), axis=1)


def above(x):
    return jnp.concatenate(split(x), axis=0)


def dot(a, b, nt=False, precision=None):
    dims = (((1,), (1 if nt else 0,)), ((), ()))
    return lax.dot_general(a, b, dims, preferred_element_type=F32, precision=precision)


def exact(a, b, nt=False):
    return dot(a, b, nt, lax.Precision.HIGHEST)


def quarters(x):
    h, w = x.shape[0] // 2, x.shape[1] // 2
    return (x[:h, :w] + x[:h, w:]) + (x[h:, :w] + x[h:, w:])


def product(x, y):
    return quarters(dot(x, y))


def kernel(
    ns, t_hbm, ops_hbm, env_hbm, assign_ref, parent_ref, out_hbm, en_ref,
    t_ref, ops_ref, env_ref, out_ref, in_sem, out_sem,
    flat, s_r, s_l, s_k, s_x, t_r, t_l, k_l, x_l, rt, lt,
    tc, lc, rc, ltc, rtc, lp, rp, ltp, rtp, kc,
    up, rs_u, u_row, u_cand, xy_row, xy,
    dp, rs_d, d_row, d_cand, dd_row, dd,
    rs_e, e_row, e_cand, e_all, ss, rs,
):
    n = lax.axis_index("node")
    s = lax.axis_index("slab")
    b = env_ref.shape[0]
    w = b // ns
    rows = pl.ds(pl.multiple_of(s * w, w), w)
    leaf = n >= 8

    loads = [
        pltpu.make_async_copy(t_hbm, t_ref, in_sem.at[0]),
        pltpu.make_async_copy(ops_hbm, ops_ref, in_sem.at[1]),
        pltpu.make_async_copy(env_hbm, env_ref, in_sem.at[2]),
    ]
    for load in loads:
        load.start()

    def block(j):
        return pl.ds(pl.multiple_of(j * w, w), w)

    c0 = jnp.where(n >= 4, 8, jnp.where(n >= 2, 4, jnp.where(n >= 1, 2, 1)))
    c1 = jnp.where(n >= 8, 8, jnp.where(n >= 1, 2 * c0, 2))
    p0 = jnp.where(n >= 8, 4, jnp.where(n >= 4, 2, jnp.where(n >= 2, 1, 0)))
    p1 = jnp.where(n >= 2, 2 * p0, jnp.where(n >= 1, 1, 0))

    barrier = pltpu.get_barrier_semaphore()

    def greet_slab(k, c):
        pl.semaphore_signal(barrier, inc=1, device_id=(n, lax.rem(s + k, ns)), device_id_type=MESH)
        return c

    def greet_node(m, c):
        pl.semaphore_signal(barrier, inc=1, device_id=(m, s), device_id_type=MESH)
        return c

    lax.fori_loop(1, ns, greet_slab, 0)
    lax.fori_loop(p0, p1, greet_node, 0)
    lax.fori_loop(c0, c1, greet_node, 0)

    @pl.when((n == 2) | (n == 3))
    def _():
        greet_node(5 - n, 0)

    pair_of_two = jnp.where((n == 2) | (n == 3), 1, 0)
    greetings = (ns - 1) + (p1 - p0) + (c1 - c0) + pair_of_two

    def peer(k):
        return lax.rem(s + 1 + lax.rem(k + ns // 2 - 2, ns - 1), ns)

    def slab_copy(q, src, dst, to, frm):
        return pltpu.make_async_remote_copy(
            src_ref=src, dst_ref=dst, send_sem=ss.at[q, to], recv_sem=rs.at[q, frm],
            device_id=(n, to), device_id_type=MESH,
        )

    def slab_start(q, src_of, dst):
        def go(k, c):
            j = peer(k)
            slab_copy(q, src_of(j), dst, j, s).start()
            return c

        lax.fori_loop(1, ns, go, 0)

    def slab_wait(q, dst_of):
        def go(k, c):
            i = lax.rem(s + k, ns)
            slab_copy(q, dst_of(i), dst_of(i), i, i).wait_recv()
            return c

        lax.fori_loop(1, ns, go, 0)

    def slab_drain(q, src_of):
        def go(k, c):
            j = lax.rem(s + k, ns)
            slab_copy(q, src_of(j), src_of(j), j, s).wait_send()
            return c

        lax.fori_loop(1, ns, go, 0)

    def node_copy(q, src, dst, to, frm):
        return pltpu.make_async_remote_copy(
            src_ref=src, dst_ref=dst, send_sem=ss.at[q, to], recv_sem=rs.at[q, frm],
            device_id=(to, s), device_id_type=MESH,
        )

    def node_start(q, src, dst, lo, hi):
        def go(m, c):
            node_copy(q, src, dst, m, n).start()
            return c

        lax.fori_loop(lo, hi, go, 0)

    def node_wait(q, dst_of, lo, hi):
        def go(m, c):
            node_copy(q, dst_of(m), dst_of(m), m, m).wait_recv()
            return c

        lax.fori_loop(lo, hi, go, 0)

    def node_drain(q, src, lo, hi):
        def go(m, c):
            node_copy(q, src, src, m, n).wait_send()
            return c

        lax.fori_loop(lo, hi, go, 0)

    def relayout(src, dst):
        for i in range(b):
            dst[i] = src[pl.ds(i, w, stride=b), :]

    def a2a_start(q, src, dst):
        slab_start(q, lambda j: src.at[block(j)], dst.at[:, rows, :])
        dst[:, rows, :] = src[rows]

    def a2a_wait(q, dst):
        slab_wait(q, lambda i: dst.at[:, block(i), :])

    def a2a_drain(q, src):
        slab_drain(q, lambda j: src.at[block(j)])

    def part(i):
        return slice(i * b, (i + 1) * b)

    def store_forms(cat, pair, i, x):
        h, l = split(x)
        cat[part(i), :] = jnp.concatenate([h, l], axis=1)
        lanes = part(i % 2)
        pair[i // 2, 0:b, lanes] = h
        pair[i // 2, b : 2 * b, lanes] = l

    def sandwich(cat, pair, x, add=None):
        side = beside(x)
        weights = jnp.concatenate([side, side], axis=0)
        total = jnp.zeros((2 * b, 2 * b), F32)
        for i in range(0, w, 2):
            moved = []
            for k in (i, i + 1):
                both = dot(cat[part(k), :], weights)
                both = both[:, :b] + both[:, b:]
                if add is not None:
                    add[k] = add[k] + both
                moved.append(above(both))
            total = total + dot(jnp.concatenate(moved, axis=1), pair[i // 2], nt=True)
        return quarters(total)

    def exact_sandwich(m, x):
        total = jnp.zeros((b, b), F32)
        for i in range(w):
            total = total + exact(exact(m[i], x), m[i], nt=True)
        return total

    def family(m):
        first = jnp.int32(NODES - 1)
        last = jnp.int32(0)
        for k in range(NODES - 1, 0, -1):
            first = jnp.where(parent_ref[k] == m, k, first)
        for k in range(1, NODES):
            last = jnp.where(parent_ref[k] == m, k, last)
        return first, last

    left_child, right_child = family(n)
    mine = parent_ref[n]
    eldest, _ = family(mine)
    side_of = jnp.where(eldest == n, 0, 1)
    first_id = assign_ref[0, n]
    second_id = assign_ref[1, n]

    loads[0].wait()

    @pl.when(n < 8)
    def _():
        for i in range(w):
            flat[part(i), :] = t_ref[part(i), :].T
        relayout(flat, s_r)

    relayout(t_ref, s_l)
    pl.semaphore_wait(barrier, greetings)

    @pl.when(n < 8)
    def _():
        a2a_start(A2A_R, s_r, t_r)

    a2a_start(A2A_L, s_l, t_l)
    loads[1].wait()
    loads[2].wait()
    op_p = ops_ref[first_id]
    op_q = ops_ref[second_id]
    for i in range(w):
        t = t_ref[part(i), :]
        tq = exact(t, op_q)
        v = jnp.where(leaf, t + tq, tq)
        flat[part(i), :] = exact(op_p, v) + jnp.where(leaf, tq, 0.0)
    relayout(flat, s_k)
    a2a_start(A2A_K, s_k, k_l)

    def right_forms():
        a2a_wait(A2A_R, t_r)
        for i in range(w):
            x = t_r[i].T
            rt[i] = x
            store_forms(rtc, rtp, i, x)
        for i in range(w):
            store_forms(rc, rp, i, t_r[i])

    def left_forms():
        a2a_wait(A2A_L, t_l)
        for i in range(w):
            x = t_l[i].T
            lt[i] = x
            store_forms(ltc, ltp, i, x)
        for i in range(w):
            store_forms(lc, lp, i, t_l[i])

    def own_forms():
        for i in range(w):
            tc[part(i), :] = beside(t_ref[part(i), :])

    def pair_square():
        a2a_wait(A2A_K, k_l)
        total = jnp.zeros((b, b), F32)
        for i in range(w):
            total = total + exact(k_l[i], t_l[i], nt=True)
        up[...] = total

    def pick_d():
        node_wait(NODE_D, lambda m: d_cand.at[m], p0, p1)
        dd_row[...] = d_cand[mine, side_of]
        slab_start(AG_D, lambda j: dd_row, dd.at[rows, :])
        dd[rows, :] = dd_row[...]

    def gather_d():
        slab_wait(AG_D, lambda i: dd.at[block(i), :])

    def push_d():
        slab_start(RS_D, lambda j: dp.at[:, block(j), :], rs_d.at[s])
        rs_d[s] = dp[:, rows, :]

    def square_d():
        d = dd[...]
        dp[0] = sandwich(rtc, rtp, d)
        dp[1] = sandwich(ltc, ltp, d)
        push_d()

    def send_d():
        slab_wait(RS_D, lambda i: rs_d.at[i])
        total = rs_d[0]
        for k in range(1, ns):
            total = total + rs_d[k]
        d_row[...] = total
        node_start(NODE_D, d_row, d_cand.at[n], c0, c1)

    def push_u():
        slab_start(RS_U, lambda j: up.at[block(j), :], rs_u.at[s])
        rs_u[s] = up[rows, :]

    def send_u():
        slab_wait(RS_U, lambda i: rs_u.at[i])
        total = rs_u[0]
        for k in range(1, ns):
            total = total + rs_u[k]
        u_row[...] = total
        node_start(NODE_U, u_row, u_cand.at[n], p0, p1)

    def pick_u():
        node_wait(NODE_U, lambda m: u_cand.at[m], c0, c1)
        xy_row[0] = u_cand[left_child]
        second = u_cand[right_child]
        xy_row[1] = jnp.where(n == 0, ops_ref[second_id, rows, :], second)
        slab_start(AG_U, lambda j: xy_row, xy.at[:, rows, :])
        xy[:, rows, :] = xy_row[...]

    def gather_u():
        slab_wait(AG_U, lambda i: xy.at[:, block(i), :])

    def square_u():
        up[...] = up[...] + (sandwich(rc, rp, xy[0]) + sandwich(lc, lp, xy[1], add=k_l))
        push_u()

    def move_left():
        x = above(xy[0])
        for i in range(w):
            flat[part(i), :] = product(x, tc[part(i), :])
        relayout(flat, s_x)
        a2a_start(A2A_X, s_x, x_l)

    def push_energy(square):
        terms = dd[...] * square
        total = terms[0:w, :]
        for k in range(1, ns):
            total = total + terms[k * w : (k + 1) * w, :]
        rs_e[s] = total
        slab_start(SLAB_E, lambda j: rs_e.at[s], rs_e.at[s])

    def own_energy():
        slab_wait(SLAB_E, lambda i: rs_e.at[i])
        total = rs_e[0]
        for k in range(1, ns):
            total = total + rs_e[k]
        return total

    def wait_total(frm):
        node_wait(NODE_F, lambda m: e_all, frm, frm + 1)

    @pl.when(leaf)
    def _():
        a2a_wait(A2A_L, t_l)
        pair_square()
        push_u()
        send_u()
        pick_d()
        gather_d()

    @pl.when((n >= 4) & (n < 8))
    def _():
        right_forms()
        left_forms()
        pair_square()
        own_forms()
        pick_u()
        gather_u()
        square_u()
        send_u()
        move_left()
        pick_d()
        gather_d()
        square_d()
        send_d()
        wait_total(2)
        node_start(NODE_F, e_all, e_all, 2 * n, 2 * n + 2)

    @pl.when((n == 2) | (n == 3))
    def _():
        right_forms()
        left_forms()
        pair_square()
        own_forms()
        pick_d()
        gather_d()
        square_d()
        pick_u()
        send_d()
        gather_u()
        square_u()
        send_u()
        push_energy(up[...])
        move_left()
        e_row[...] = own_energy()
        e_cand[n] = e_row[...]
        node_start(NODE_E, e_row, e_cand.at[n], 5 - n, 6 - n)
        node_wait(NODE_E, lambda m: e_cand.at[m], 1, 2)
        node_wait(NODE_E, lambda m: e_cand.at[m], 5 - n, 6 - n)
        e_all[...] = e_cand[1] + (e_cand[2] + e_cand[3])

        @pl.when(n == 2)
        def _():
            node_start(NODE_F, e_all, e_all, 4, 8)
            node_start(NODE_F, e_all, e_all, 1, 2)

    @pl.when(n == 1)
    def _():
        right_forms()
        left_forms()
        pick_d()
        gather_d()
        d = dd[...]
        dp[0] = exact_sandwich(rt, d)
        dp[1] = exact_sandwich(lt, d)
        push_d()
        send_d()
        pair_square()
        push_energy(up[...])
        own_forms()
        own = own_energy()
        node_wait(NODE_E, lambda m: e_cand.at[m], 0, 1)
        e_row[...] = own + e_cand[0]
        node_start(NODE_E, e_row, e_cand.at[n], 2, 4)
        pick_u()
        gather_u()
        square_u()
        send_u()
        move_left()
        wait_total(2)
        node_start(NODE_F, e_all, e_all, 0, 1)

    @pl.when(n == 0)
    def _():
        dd[...] = env_ref[...]
        right_forms()
        dp[0] = exact_sandwich(rt, env_ref[...])
        dp[1] = jnp.zeros((b, b), F32)
        push_d()
        send_d()
        left_forms()
        pair_square()
        push_energy(up[...] + sandwich(lc, lp, op_q, add=k_l))
        e_row[...] = own_energy()
        node_start(NODE_E, e_row, e_cand.at[n], 1, 2)
        own_forms()
        pick_u()
        gather_u()
        move_left()
        wait_total(1)

    factor = b**0.75

    @pl.when(n < 8)
    def _():
        a2a_wait(A2A_X, x_l)

    for i in range(w):
        kc[part(i), :] = beside(k_l[i] + jnp.where(n < 8, x_l[i], 0.0))
    chunk = b // 2
    puts = []
    for h in range(2):
        d = above(dd[h * chunk : (h + 1) * chunk, :] * factor)
        for i in range(w):
            out_ref[pl.ds(h * chunk * w + i, chunk, stride=w), :] = product(d, kc[part(i), :])
        span = pl.ds(h * chunk * w, chunk * w)
        puts.append(pltpu.make_async_copy(out_ref.at[span, :], out_hbm.at[span, :], out_sem.at[h]))
        puts[h].start()

    @pl.when(leaf)
    def _():
        wait_total(n // 2)

    en_ref[...] = jnp.sum(e_all[...], axis=(0, 1), keepdims=True)

    a2a_drain(A2A_L, s_l)
    a2a_drain(A2A_K, s_k)

    @pl.when(n < 8)
    def _():
        a2a_drain(A2A_R, s_r)
        a2a_drain(A2A_X, s_x)
        slab_drain(RS_D, lambda j: dp.at[:, block(j), :])
        node_drain(NODE_D, d_row, c0, c1)
        slab_drain(AG_U, lambda j: xy_row)

    @pl.when(n >= 1)
    def _():
        slab_drain(RS_U, lambda j: up.at[block(j), :])
        node_drain(NODE_U, u_row, p0, p1)
        slab_drain(AG_D, lambda j: dd_row)

    @pl.when(n < 4)
    def _():
        slab_drain(SLAB_E, lambda j: rs_e.at[s])
        node_drain(NODE_E, e_row, jnp.where(n >= 2, 5 - n, n + 1), jnp.where(n >= 2, 6 - n, 2 * n + 2))

    @pl.when(n == 1)
    def _():
        node_drain(NODE_F, e_all, 0, 1)

    @pl.when(n == 2)
    def _():
        node_drain(NODE_F, e_all, 4, 8)
        node_drain(NODE_F, e_all, 1, 2)

    @pl.when((n >= 4) & (n < 8))
    def _():
        node_drain(NODE_F, e_all, 2 * n, 2 * n + 2)

    for put in puts:
        put.wait()


def per_device(ns, tensors, ops, assign, parent, env):
    b = env.shape[0]
    w = b // ns
    stack = pltpu.VMEM((w * b, b), F32)
    full = pltpu.VMEM((b, w, b), F32)
    form = pltpu.VMEM((w, b, b), F32)
    cat = pltpu.VMEM((w * b, 2 * b), BF16)
    pair = pltpu.VMEM((w // 2, 2 * b, 2 * b), BF16)
    square = pltpu.VMEM((b, b), F32)
    slab = pltpu.VMEM((w, b), F32)
    two = pltpu.VMEM((2, w, b), F32)
    slots = max(ns, NODES)
    smem = pl.BlockSpec(memory_space=pltpu.SMEM)
    hbm = pl.BlockSpec(memory_space=pl.ANY)
    grad, energy = pl.pallas_call(
        functools.partial(kernel, ns),
        out_shape=(jax.ShapeDtypeStruct((b * w, b), F32), jax.ShapeDtypeStruct((1, 1), F32)),
        in_specs=[hbm, hbm, hbm, smem, smem],
        out_specs=(hbm, pl.BlockSpec(memory_space=pltpu.VMEM)),
        scratch_shapes=[
            stack, pltpu.VMEM(ops.shape, F32), square, stack,
            pltpu.SemaphoreType.DMA((3,)), pltpu.SemaphoreType.DMA((2,)),
            stack, full, full, full, full, form, form, form, form, form, form,
            cat, cat, cat, cat, cat, pair, pair, pair, pair, cat,
            square, pltpu.VMEM((ns, w, b), F32), slab, pltpu.VMEM((NODES, w, b), F32), two, pltpu.VMEM((2, b, b), F32),
            pltpu.VMEM((2, b, b), F32), pltpu.VMEM((ns, 2, w, b), F32), two,
            pltpu.VMEM((NODES, 2, w, b), F32), slab, square,
            pltpu.VMEM((ns, w, b), F32), slab, pltpu.VMEM((NODES, w, b), F32), slab,
            pltpu.SemaphoreType.DMA((13, slots)), pltpu.SemaphoreType.DMA((13, slots)),
        ],
        compiler_params=pltpu.CompilerParams(collective_id=0, has_side_effects=True),
    )(tensors.reshape(w * b, b), ops, env, assign.T, parent)
    return grad.reshape(1, b, w, b), energy[0, 0]


def solution(mesh):
    return jax.shard_map(
        functools.partial(per_device, mesh.shape["slab"]),
        mesh=mesh,
        in_specs=(P("node", "slab", None, None), P(), P(), P(), P()),
        out_specs=(P("node", None, "slab", None), P()),
        check_vma=False,
    )
```

time: 115 us -> 101 us (0.88)
  Pallas kernels: 108 us -> 97 us
  local copies, waits for them, and re-layouts: 3.49 us -> 1.87 us
    pallas_call x1, Pallas kernels: 108 us -> 97 us  [per_device(): pl.pallas_call(functools.partial(kernel, ns), out_shape=(jax.ShapeDtypeSt...]
    unnamed x4 -> x1, local copies, waits for them, and re-layouts: 3.49 us -> 1.87 us
where the time goes in v2:
time: 101 us
  Pallas kernels  97 us (96%)
  between operations  2.34 us (2%)
  local copies, waits for them, and re-layouts  1.87 us (2%)
    pallas_call x1, Pallas kernels, per_device(): pl.pallas_call(functools.partial(kernel, ns), out_shape=(jax.ShapeDtypeSt...  97 us

profile of v2, /device:TPU:1, one launch (start us, length us, event | category | flops | bytes accessed | tf_op | source)
XLA Modules:
  0.0 101.2 jit_solution(17194804053950815999)
XLA Ops:
  0.6 97.0 %shard_map.68 = (f32[1024,128]{1,0:T(8,128)}, f32[1,1]{1,0:T(1,128)}) custom-call(f32[1024,128]{1,0:T(8,128)} %bitcast.4, f32[8,128,128]{2,1,0:T(8,128)} %ops_hbm.1, f32[128,128]{1,0:T(8,128)} %env_hbm.1, s32[2,16]{1,0:T(2,128)} %bitcast.6, s32[16]{0:T(128)} %parent_ref.1), custom_call_target="tpu_custom_call" | custom-call | tf_op jit(solution)/shard_map/pallas_call | solution.py:536
  97.6 1.9 %copy.9 = f32[1,128,8,128]{3,2,1,0:T(8,128)} copy(f32[1,128,8,128]{3,2,1,0:T(8,128)} %bitcast.5) | data formatting | bytes 1048576

commit v3 on v2

--- a/solution.py
+++ b/solution.py
@@ -12,7 +12,7 @@
 F32 = jnp.float32
 BF16 = jnp.bfloat16
 
-A2A_R, A2A_L, A2A_K, A2A_X, RS_U, RS_D, AG_U, AG_D, SLAB_E, NODE_U, NODE_D, NODE_E, NODE_F = range(13)
+A2A_R, A2A_L, A2A_K, A2A_X, RS_U, RS_D, AG_U, AG_D, SLAB_E, NODE_U, NODE_D, NODE_E, NODE_F, A2A_Z, MERGE, MERGE2 = range(16)
 
 
 def split(x):
@@ -47,10 +47,10 @@
 
 
 def kernel(
-    ns, t_hbm, ops_hbm, env_hbm, assign_ref, parent_ref, out_hbm, en_ref,
-    t_ref, ops_ref, env_ref, out_ref, in_sem, out_sem,
-    flat, s_r, s_l, s_k, s_x, t_r, t_l, k_l, x_l, rt, lt,
-    tc, lc, rc, ltc, rtc, lp, rp, ltp, rtp, kc,
+    ns, t_hbm, ops_hbm, env_hbm, assign_ref, parent_ref, out_ref, en_ref,
+    t_ref, ops_ref, env_ref, in_sem,
+    s_r, s_l, s_k, s_x, t_r, t_l, k_l, x_l, rt, lt,
+    tc, lc, rc, ltc, rtc, m_u,
     up, rs_u, u_row, u_cand, xy_row, xy,
     dp, rs_d, d_row, d_cand, dd_row, dd,
     rs_e, e_row, e_cand, e_all, ss, rs,
@@ -90,14 +90,26 @@
 
     lax.fori_loop(1, ns, greet_slab, 0)
     lax.fori_loop(p0, p1, greet_node, 0)
-    lax.fori_loop(c0, c1, greet_node, 0)
+
+    @pl.when(n >= 2)
+    def _():
+        lax.fori_loop(c0, c1, greet_node, 0)
+
+    @pl.when(n < 2)
+    def _():
+        def greet_all(k, c):
+            m = c0 + k // ns
+            pl.semaphore_signal(barrier, inc=1, device_id=(m, lax.rem(k, ns)), device_id_type=MESH)
+            return c
+
+        lax.fori_loop(0, (c1 - c0) * ns, greet_all, 0)
 
     @pl.when((n == 2) | (n == 3))
     def _():
         greet_node(5 - n, 0)
 
     pair_of_two = jnp.where((n == 2) | (n == 3), 1, 0)
-    greetings = (ns - 1) + (p1 - p0) + (c1 - c0) + pair_of_two
+    greetings = (ns - 1) + jnp.where((n >= 1) & (n < 4), ns, p1 - p0) + (c1 - c0) + pair_of_two
 
     def peer(k):
         return lax.rem(s + 1 + lax.rem(k + ns // 2 - 2, ns - 1), ns)
@@ -159,9 +171,8 @@
 
         lax.fori_loop(lo, hi, go, 0)
 
-    def relayout(src, dst):
-        for i in range(b):
-            dst[i] = src[pl.ds(i, w, stride=b), :]
+    def spread(dst, i, x):
+        dst.reshape(b * w, b)[pl.ds(i, b, stride=w), :] = x
 
     def a2a_start(q, src, dst):
         slab_start(q, lambda j: src.at[block(j)], dst.at[:, rows, :])
@@ -176,14 +187,7 @@
     def part(i):
         return slice(i * b, (i + 1) * b)
 
-    def store_forms(cat, pair, i, x):
-        h, l = split(x)
-        cat[part(i), :] = jnp.concatenate([h, l], axis=1)
-        lanes = part(i % 2)
-        pair[i // 2, 0:b, lanes] = h
-        pair[i // 2, b : 2 * b, lanes] = l
-
-    def sandwich(cat, pair, x, add=None):
+    def sandwich(cat, turned, x, add=None):
         side = beside(x)
         weights = jnp.concatenate([side, side], axis=0)
         total = jnp.zeros((2 * b, 2 * b), F32)
@@ -195,7 +199,7 @@
                 if add is not None:
                     add[k] = add[k] + both
                 moved.append(above(both))
-            total = total + dot(jnp.concatenate(moved, axis=1), pair[i // 2], nt=True)
+            total = total + dot(jnp.concatenate(moved, axis=1), turned[i * b : (i + 2) * b, :])
         return quarters(total)
 
     def exact_sandwich(m, x):
@@ -225,10 +229,10 @@
     @pl.when(n < 8)
     def _():
         for i in range(w):
-            flat[part(i), :] = t_ref[part(i), :].T
-        relayout(flat, s_r)
-
-    relayout(t_ref, s_l)
+            spread(s_r, i, t_ref[part(i), :].T)
+
+    for i in range(w):
+        spread(s_l, i, t_ref[part(i), :])
     pl.semaphore_wait(barrier, greetings)
 
     @pl.when(n < 8)
@@ -244,8 +248,7 @@
         t = t_ref[part(i), :]
         tq = exact(t, op_q)
         v = jnp.where(leaf, t + tq, tq)
-        flat[part(i), :] = exact(op_p, v) + jnp.where(leaf, tq, 0.0)
-    relayout(flat, s_k)
+        spread(s_k, i, exact(op_p, v) + jnp.where(leaf, tq, 0.0))
     a2a_start(A2A_K, s_k, k_l)
 
     def right_forms():
@@ -253,18 +256,18 @@
         for i in range(w):
             x = t_r[i].T
             rt[i] = x
-            store_forms(rtc, rtp, i, x)
-        for i in range(w):
-            store_forms(rc, rp, i, t_r[i])
+            rtc[part(i), :] = beside(x)
+        for i in range(w):
+            rc[part(i), :] = beside(t_r[i])
 
     def left_forms():
         a2a_wait(A2A_L, t_l)
         for i in range(w):
             x = t_l[i].T
             lt[i] = x
-            store_forms(ltc, ltp, i, x)
-        for i in range(w):
-            store_forms(lc, lp, i, t_l[i])
+            ltc[part(i), :] = beside(x)
+        for i in range(w):
+            lc[part(i), :] = beside(t_l[i])
 
     def own_forms():
         for i in range(w):
@@ -292,8 +295,8 @@
 
     def square_d():
         d = dd[...]
-        dp[0] = sandwich(rtc, rtp, d)
-        dp[1] = sandwich(ltc, ltp, d)
+        dp[0] = sandwich(rtc, rc, d)
+        dp[1] = sandwich(ltc, lc, d)
         push_d()
 
     def send_d():
@@ -316,26 +319,58 @@
         u_row[...] = total
         node_start(NODE_U, u_row, u_cand.at[n], p0, p1)
 
+    def spread_u():
+        slab_start(AG_U, lambda j: xy_row, xy.at[:, rows, :])
+        xy[:, rows, :] = xy_row[...]
+
     def pick_u():
         node_wait(NODE_U, lambda m: u_cand.at[m], c0, c1)
         xy_row[0] = u_cand[left_child]
-        second = u_cand[right_child]
-        xy_row[1] = jnp.where(n == 0, ops_ref[second_id, rows, :], second)
-        slab_start(AG_U, lambda j: xy_row, xy.at[:, rows, :])
-        xy[:, rows, :] = xy_row[...]
+        xy_row[1] = u_cand[right_child]
+        spread_u()
+
+    def merged_copy(src, slot, owner, to, frm):
+        return pltpu.make_async_remote_copy(
+            src_ref=src, dst_ref=m_u.at[slot, frm], send_sem=ss.at[MERGE, owner], recv_sem=rs.at[MERGE + slot, frm],
+            device_id=(to, owner), device_id_type=MESH,
+        )
+
+    def push_merged():
+        def go(k, c):
+            j = lax.rem(s + k + ns // 2, ns)
+            merged_copy(up.at[block(j), :], jnp.where(n == 3, 1, 0), j, n // 2, s).start()
+            return c
+
+        lax.fori_loop(0, ns, go, 0)
+
+    def drain_merged():
+        def go(j, c):
+            merged_copy(up.at[block(j), :], 0, j, n // 2, s).wait_send()
+            return c
+
+        lax.fori_loop(0, ns, go, 0)
+
+    def pick_merged(slot):
+        def go(i, c):
+            merged_copy(m_u.at[slot, i], slot, i, n, i).wait_recv()
+            return c
+
+        lax.fori_loop(0, ns, go, 0)
+        total = m_u[slot, 0]
+        for k in range(1, ns):
+            total = total + m_u[slot, k]
+        xy_row[slot] = total
 
     def gather_u():
         slab_wait(AG_U, lambda i: xy.at[:, block(i), :])
 
     def square_u():
-        up[...] = up[...] + (sandwich(rc, rp, xy[0]) + sandwich(lc, lp, xy[1], add=k_l))
-        push_u()
+        up[...] = up[...] + (sandwich(rc, rtc, xy[0]) + sandwich(lc, ltc, xy[1], add=k_l))
 
     def move_left():
         x = above(xy[0])
         for i in range(w):
-            flat[part(i), :] = product(x, tc[part(i), :])
-        relayout(flat, s_x)
+            spread(s_x, i, product(x, tc[part(i), :]))
         a2a_start(A2A_X, s_x, x_l)
 
     def push_energy(square):
@@ -356,12 +391,23 @@
     def wait_total(frm):
         node_wait(NODE_F, lambda m: e_all, frm, frm + 1)
 
+    def drain_first():
+        a2a_drain(A2A_L, s_l)
+        a2a_drain(A2A_K, s_k)
+
+        @pl.when(n < 8)
+        def _():
+            a2a_drain(A2A_R, s_r)
+
+    factor = b**0.75
+
     @pl.when(leaf)
     def _():
         a2a_wait(A2A_L, t_l)
         pair_square()
         push_u()
         send_u()
+        drain_first()
         pick_d()
         gather_d()
 
@@ -374,8 +420,10 @@
         pick_u()
         gather_u()
         square_u()
+        push_u()
         send_u()
         move_left()
+        drain_first()
         pick_d()
         gather_d()
         square_d()
@@ -389,6 +437,7 @@
         left_forms()
         pair_square()
         own_forms()
+        drain_first()
         pick_d()
         gather_d()
         square_d()
@@ -396,7 +445,7 @@
         send_d()
         gather_u()
         square_u()
-        send_u()
+        push_merged()
         push_energy(up[...])
         move_left()
         e_row[...] = own_energy()
@@ -429,10 +478,13 @@
         node_wait(NODE_E, lambda m: e_cand.at[m], 0, 1)
         e_row[...] = own + e_cand[0]
         node_start(NODE_E, e_row, e_cand.at[n], 2, 4)
-        pick_u()
+        drain_first()
+        pick_merged(0)
+        pick_merged(1)
+        spread_u()
         gather_u()
         square_u()
-        send_u()
+        push_merged()
         move_left()
         wait_total(2)
         node_start(NODE_F, e_all, e_all, 0, 1)
@@ -446,33 +498,55 @@
         push_d()
         send_d()
         left_forms()
+        d = above(env_ref[...] * factor)
+        for i in range(w):
+            x_l[i] = product(d, lc[part(i), :])
+        slab_start(A2A_Z, lambda j: x_l.at[:, block(j), :], s_x.at[rows])
+        s_x[rows] = x_l[:, rows, :]
         pair_square()
-        push_energy(up[...] + sandwich(lc, lp, op_q, add=k_l))
+        push_energy(up[...] + sandwich(lc, ltc, op_q))
         e_row[...] = own_energy()
         node_start(NODE_E, e_row, e_cand.at[n], 1, 2)
-        own_forms()
-        pick_u()
-        gather_u()
-        move_left()
+        slab_wait(A2A_Z, lambda i: s_x.at[block(i)])
+        q_side = beside(op_q)
+        q_weights = jnp.concatenate([q_side, q_side], axis=0)
+        p_above = above(op_p)
+        for i in range(w):
+            side = beside(s_x.reshape(b * w, b)[pl.ds(i, b, stride=w), :])
+            tc[part(i), :] = side
+            moved = dot(side, q_weights)
+            moved = moved[:, :b] + moved[:, b:]
+            t_r[i] = product(p_above, beside(moved)) + moved
+        drain_first()
+        slab_drain(A2A_Z, lambda j: x_l.at[:, block(j), :])
+        slab_drain(RS_D, lambda j: dp.at[:, block(j), :])
+        node_drain(NODE_D, d_row, c0, c1)
+        slab_drain(SLAB_E, lambda j: rs_e.at[s])
+        node_drain(NODE_E, e_row, 1, 2)
+        pick_merged(0)
+        slab_start(AG_U, lambda j: xy_row.at[0], xy.at[0, rows, :])
+        xy[0, rows, :] = xy_row[0]
+        slab_wait(AG_U, lambda i: xy.at[0, block(i), :])
+        x = above(xy[0])
+        for i in range(w):
+            k_l[i] = product(x, tc[part(i), :]) + t_r[i]
+        slab_start(A2A_X, lambda j: k_l.at[:, block(j), :], out_ref.at[rows])
+        out_ref[rows] = k_l[:, rows, :]
         wait_total(1)
-
-    factor = b**0.75
-
-    @pl.when(n < 8)
-    def _():
-        a2a_wait(A2A_X, x_l)
-
-    for i in range(w):
-        kc[part(i), :] = beside(k_l[i] + jnp.where(n < 8, x_l[i], 0.0))
-    chunk = b // 2
-    puts = []
-    for h in range(2):
-        d = above(dd[h * chunk : (h + 1) * chunk, :] * factor)
-        for i in range(w):
-            out_ref[pl.ds(h * chunk * w + i, chunk, stride=w), :] = product(d, kc[part(i), :])
-        span = pl.ds(h * chunk * w, chunk * w)
-        puts.append(pltpu.make_async_copy(out_ref.at[span, :], out_hbm.at[span, :], out_sem.at[h]))
-        puts[h].start()
+        slab_drain(AG_U, lambda j: xy_row.at[0])
+        slab_wait(A2A_X, lambda i: out_ref.at[block(i)])
+        slab_drain(A2A_X, lambda j: k_l.at[:, block(j), :])
+
+    @pl.when(n >= 1)
+    def _():
+        @pl.when(n < 8)
+        def _():
+            a2a_wait(A2A_X, x_l)
+
+        d = above(dd[...] * factor)
+        for i in range(w):
+            side = beside(k_l[i] + jnp.where(n < 8, x_l[i], 0.0))
+            out_ref.reshape(b * w, b)[pl.ds(i, b, stride=w), :] = product(d, side)
 
     @pl.when(leaf)
     def _():
@@ -480,12 +554,8 @@
 
     en_ref[...] = jnp.sum(e_all[...], axis=(0, 1), keepdims=True)
 
-    a2a_drain(A2A_L, s_l)
-    a2a_drain(A2A_K, s_k)
-
-    @pl.when(n < 8)
-    def _():
-        a2a_drain(A2A_R, s_r)
+    @pl.when((n >= 1) & (n < 8))
+    def _():
         a2a_drain(A2A_X, s_x)
         slab_drain(RS_D, lambda j: dp.at[:, block(j), :])
         node_drain(NODE_D, d_row, c0, c1)
@@ -493,12 +563,16 @@
 
     @pl.when(n >= 1)
     def _():
+        slab_drain(AG_D, lambda j: dd_row)
+
+    @pl.when(n >= 4)
+    def _():
         slab_drain(RS_U, lambda j: up.at[block(j), :])
         node_drain(NODE_U, u_row, p0, p1)
-        slab_drain(AG_D, lambda j: dd_row)
-
-    @pl.when(n < 4)
-    def _():
+
+    @pl.when((n >= 1) & (n < 4))
+    def _():
+        drain_merged()
         slab_drain(SLAB_E, lambda j: rs_e.at[s])
         node_drain(NODE_E, e_row, jnp.where(n >= 2, 5 - n, n + 1), jnp.where(n >= 2, 6 - n, 2 * n + 2))
 
@@ -514,9 +588,6 @@
     @pl.when((n >= 4) & (n < 8))
     def _():
         node_drain(NODE_F, e_all, 2 * n, 2 * n + 2)
-
-    for put in puts:
-        put.wait()
 
 
 def per_device(ns, tensors, ops, assign, parent, env):
@@ -526,32 +597,31 @@
     full = pltpu.VMEM((b, w, b), F32)
     form = pltpu.VMEM((w, b, b), F32)
     cat = pltpu.VMEM((w * b, 2 * b), BF16)
-    pair = pltpu.VMEM((w // 2, 2 * b, 2 * b), BF16)
     square = pltpu.VMEM((b, b), F32)
     slab = pltpu.VMEM((w, b), F32)
     two = pltpu.VMEM((2, w, b), F32)
     slots = max(ns, NODES)
     smem = pl.BlockSpec(memory_space=pltpu.SMEM)
     hbm = pl.BlockSpec(memory_space=pl.ANY)
+    vmem = pl.BlockSpec(memory_space=pltpu.VMEM)
     grad, energy = pl.pallas_call(
         functools.partial(kernel, ns),
-        out_shape=(jax.ShapeDtypeStruct((b * w, b), F32), jax.ShapeDtypeStruct((1, 1), F32)),
+        out_shape=(pltpu.VMEM((b, w, b), F32), jax.ShapeDtypeStruct((1, 1), F32)),
         in_specs=[hbm, hbm, hbm, smem, smem],
-        out_specs=(hbm, pl.BlockSpec(memory_space=pltpu.VMEM)),
+        out_specs=(vmem, vmem),
         scratch_shapes=[
-            stack, pltpu.VMEM(ops.shape, F32), square, stack,
-            pltpu.SemaphoreType.DMA((3,)), pltpu.SemaphoreType.DMA((2,)),
-            stack, full, full, full, full, form, form, form, form, form, form,
-            cat, cat, cat, cat, cat, pair, pair, pair, pair, cat,
+            stack, pltpu.VMEM(ops.shape, F32), square, pltpu.SemaphoreType.DMA((3,)),
+            full, full, full, full, form, form, form, form, form, form,
+            cat, cat, cat, cat, cat, pltpu.VMEM((2, ns, w, b), F32),
             square, pltpu.VMEM((ns, w, b), F32), slab, pltpu.VMEM((NODES, w, b), F32), two, pltpu.VMEM((2, b, b), F32),
             pltpu.VMEM((2, b, b), F32), pltpu.VMEM((ns, 2, w, b), F32), two,
             pltpu.VMEM((NODES, 2, w, b), F32), slab, square,
             pltpu.VMEM((ns, w, b), F32), slab, pltpu.VMEM((NODES, w, b), F32), slab,
-            pltpu.SemaphoreType.DMA((13, slots)), pltpu.SemaphoreType.DMA((13, slots)),
+            pltpu.SemaphoreType.DMA((16, slots)), pltpu.SemaphoreType.DMA((16, slots)),
         ],
         compiler_params=pltpu.CompilerParams(collective_id=0, has_side_effects=True),
     )(tensors.reshape(w * b, b), ops, env, assign.T, parent)
-    return grad.reshape(1, b, w, b), energy[0, 0]
+    return grad[None], energy[0, 0]
 
 
 def solution(mesh):

time: 101 us -> 95.5 us (0.946)
  Pallas kernels: 97 us -> 92.2 us
  local copies, waits for them, and re-layouts: 1.87 us -> 0.8 us
    pallas_call x1, Pallas kernels: 97 us -> 92.2 us  [per_device(): pl.pallas_call(functools.partial(kernel, ns), out_shape=(pltpu.VMEM((b, w...]
    unnamed x1, local copies, waits for them, and re-layouts: 1.87 us -> 0.8 us
where the time goes in v3:
time: 95.5 us; the launch traced here: 95.4 us
  Pallas kernels  92.2 us (97%)
  between operations  2.33 us (2%)
    pallas_call x1, Pallas kernels, per_device(): pl.pallas_call(functools.partial(kernel, ns), out_shape=(pltpu.VMEM((b, w...  92.2 us

profile of v3, /device:TPU:1, one launch (start us, length us, event | category | flops | bytes accessed | tf_op | source)
XLA Modules:
  0.0 95.4 jit_solution(6596751705768527787)
XLA Ops:
  0.6 92.2 %shard_map.68 = (f32[128,8,128]{2,1,0:T(8,128)S(1)}, f32[1,1]{1,0:T(1,128)}) custom-call(f32[1024,128]{1,0:T(8,128)} %bitcast.5, f32[8,128,128]{2,1,0:T(8,128)} %ops_hbm.1, f32[128,128]{1,0:T(8,128)} %env_hbm.1, s32[2,16]{1,0:T(2,128)} %bitcast.6, s32[16]{0:T(128)} %parent_ref.1), custom_call_target="tpu_custom_call" | custom-call | tf_op jit(solution)/shard_map/pallas_call | solution.py:607
  92.9 0.8 copy.9

commit v4 on v3

v4 whole, which is shorter than its diff:
```python
import functools

import jax
import jax.numpy as jnp
from jax import lax
from jax.experimental import pallas as pl
from jax.experimental.pallas import tpu as pltpu
from jax.sharding import PartitionSpec as P

NODES = 16
MESH = pl.DeviceIdType.MESH
F32 = jnp.float32
BF16 = jnp.bfloat16

A2A_R, A2A_L, A2A_K, A2A_X, RS_U, RS_D, AG_U, AG_D, SLAB_E, NODE_U, NODE_D, NODE_E, NODE_F, A2A_Z, MERGE, MERGE2, COPIES, COUNT = range(18)


def split(x):
    hi = x.astype(BF16)
    return hi, (x - hi.astype(F32)).astype(BF16)


def beside(x):
    return jnp.concatenate(split(x), axis=1)


def above(x):
    return jnp.concatenate(split(x), axis=0)


def dot(a, b, nt=False, precision=None):
    dims = (((1,), (1 if nt else 0,)), ((), ()))
    return lax.dot_general(a, b, dims, preferred_element_type=F32, precision=precision)


def exact(a, b, nt=False):
    return dot(a, b, nt, lax.Precision.HIGHEST)


def quarters(x):
    h, w = x.shape[0] // 2, x.shape[1] // 2
    return (x[:h, :w] + x[:h, w:]) + (x[h:, :w] + x[h:, w:])


def product(x, y):
    return quarters(dot(x, y))


def kernel(
    ns, t_hbm, ops_hbm, env_hbm, assign_hbm, parent_hbm, out_ref, en_ref,
    t_ref, ops_ref, env_ref, assign_ref, parent_ref, in_sem,
    s_r, s_l, s_k, s_x, t_r, t_l, k_l, x_l, rt, lt,
    tc, lc, rc, ltc, rtc, m_u,
    up, rs_u, u_row, u_cand, xy_row, xy,
    dp, rs_d, d_row, d_cand, dd_row, dd,
    rs_e, e_row, e_cand, e_all, z, zc, base, gb, x_near, p_one, ss, rs,
):
    n = lax.axis_index("node")
    s = lax.axis_index("slab")
    b = env_ref.shape[0]
    w = b // ns
    rows = pl.ds(pl.multiple_of(s * w, w), w)
    leaf = n >= 8

    loads = [
        pltpu.make_async_copy(t_hbm, t_ref, in_sem.at[0]),
        pltpu.make_async_copy(ops_hbm, ops_ref, in_sem.at[1]),
        pltpu.make_async_copy(env_hbm, env_ref, in_sem.at[2]),
        pltpu.make_async_copy(assign_hbm, assign_ref, in_sem.at[3]),
        pltpu.make_async_copy(parent_hbm, parent_ref, in_sem.at[4]),
    ]
    for load in (loads[0], loads[3], loads[4]):
        load.start()

    def block(j):
        return pl.ds(pl.multiple_of(j * w, w), w)

    c0 = jnp.where(n >= 4, 8, jnp.where(n >= 2, 4, jnp.where(n >= 1, 2, 1)))
    c1 = jnp.where(n >= 8, 8, jnp.where(n >= 1, 2 * c0, 2))
    p0 = jnp.where(n >= 8, 4, jnp.where(n >= 4, 2, jnp.where(n >= 2, 1, 0)))
    p1 = jnp.where(n >= 2, 2 * p0, jnp.where(n >= 1, 1, 0))

    barrier = pltpu.get_barrier_semaphore()

    def greet_slab(k, c):
        pl.semaphore_signal(barrier, inc=1, device_id=(n, lax.rem(s + k, ns)), device_id_type=MESH)
        return c

    def greet_node(m, c):
        pl.semaphore_signal(barrier, inc=1, device_id=(m, s), device_id_type=MESH)
        return c

    lax.fori_loop(1, ns, greet_slab, 0)
    lax.fori_loop(p0, p1, greet_node, 0)

    @pl.when(n >= 2)
    def _():
        lax.fori_loop(c0, c1, greet_node, 0)

    @pl.when(n < 2)
    def _():
        def greet_all(k, c):
            m = c0 + k // ns
            pl.semaphore_signal(barrier, inc=1, device_id=(m, lax.rem(k, ns)), device_id_type=MESH)
            return c

        lax.fori_loop(0, (c1 - c0) * ns, greet_all, 0)

    @pl.when((n == 2) | (n == 3))
    def _():
        greet_node(5 - n, 0)

    pair_of_two = jnp.where((n == 2) | (n == 3), 1, 0)
    greetings = (ns - 1) + jnp.where((n >= 1) & (n < 4), ns, p1 - p0) + (c1 - c0) + pair_of_two

    def peer(k):
        return lax.rem(s + 1 + lax.rem(k + ns // 2 - 2, ns - 1), ns)

    def remote(q, src, dst, to, slab, arrival=None):
        return pltpu.make_async_remote_copy(
            src_ref=src, dst_ref=dst, send_sem=ss.at[q], recv_sem=rs.at[q if arrival is None else arrival],
            device_id=(to, slab), device_id_type=MESH,
        )

    def arrived(q, like):
        remote(q, like, like, n, lax.rem(s + 1, ns)).wait_recv()

    def drained(q, like):
        remote(q, like, like, n, lax.rem(s + 1, ns)).wait_send()

    def slab_start(q, src_of, dst):
        def go(k, c):
            j = peer(k)
            remote(q, src_of(j), dst, n, j).start()
            return c

        lax.fori_loop(1, ns, go, 0)

    def node_start(q, src, dst, lo, hi):
        def go(m, c):
            remote(q, src, dst, m, s).start()
            return c

        lax.fori_loop(lo, hi, go, 0)

    others = pl.ds(0, ns - 1)
    other_rows = pl.ds(0, b - w)

    def spread(dst, i, x):
        dst.reshape(b * w, b)[pl.ds(i, b, stride=w), :] = x

    def a2a_start(q, src, dst):
        slab_start(q, lambda j: src.at[block(j)], dst.at[:, rows, :])
        dst[:, rows, :] = src[rows]

    def a2a_wait(q, dst):
        arrived(q, dst.at[:, other_rows, :])

    def a2a_drain(q, src):
        drained(q, src.at[other_rows])

    def part(i):
        return slice(i * b, (i + 1) * b)

    def sandwich(cat, turned, x, add=None):
        side = beside(x)
        weights = jnp.concatenate([side, side], axis=0)
        total = jnp.zeros((2 * b, 2 * b), F32)
        for i in range(0, w, 2):
            moved = []
            for k in (i, i + 1):
                both = dot(cat[part(k), :], weights)
                both = both[:, :b] + both[:, b:]
                if add is not None:
                    add[k] = add[k] + both
                moved.append(above(both))
            total = total + dot(jnp.concatenate(moved, axis=1), turned[i * b : (i + 2) * b, :])
        return quarters(total)

    def exact_sandwich(m, x):
        total = jnp.zeros((b, b), F32)
        for i in range(w):
            total = total + exact(exact(m[i], x), m[i], nt=True)
        return total

    def family(m):
        first = jnp.int32(NODES - 1)
        last = jnp.int32(0)
        for k in range(NODES - 1, 0, -1):
            first = jnp.where(parent_ref[k] == m, k, first)
        for k in range(1, NODES):
            last = jnp.where(parent_ref[k] == m, k, last)
        return first, last

    loads[0].wait()
    loads[1].start()
    loads[2].start()

    @pl.when(n < 8)
    def _():
        for i in range(w):
            spread(s_r, i, t_ref[part(i), :].T)

    for i in range(w):
        spread(s_l, i, t_ref[part(i), :])
    pl.semaphore_wait(barrier, greetings)

    @pl.when(n < 8)
    def _():
        a2a_start(A2A_R, s_r, t_r)

    a2a_start(A2A_L, s_l, t_l)
    for load in loads[1:]:
        load.wait()
    left_child, right_child = family(n)
    mine = parent_ref[n]
    eldest, _ = family(mine)
    side_of = jnp.where(eldest == n, 0, 1)
    first_id = assign_ref[0, n]
    second_id = assign_ref[1, n]
    op_p = ops_ref[first_id]
    op_q = ops_ref[second_id]
    for i in range(w):
        t = t_ref[part(i), :]
        tq = exact(t, op_q)
        v = jnp.where(leaf, t + tq, tq)
        spread(s_k, i, exact(op_p, v) + jnp.where(leaf, tq, 0.0))
    a2a_start(A2A_K, s_k, k_l)

    def right_forms():
        a2a_wait(A2A_R, t_r)
        for i in range(w):
            x = t_r[i].T
            rt[i] = x
            rtc[part(i), :] = beside(x)
        for i in range(w):
            rc[part(i), :] = beside(t_r[i])

    def left_forms():
        a2a_wait(A2A_L, t_l)
        for i in range(w):
            x = t_l[i].T
            lt[i] = x
            ltc[part(i), :] = beside(x)
        for i in range(w):
            lc[part(i), :] = beside(t_l[i])

    def own_forms():
        for i in range(w):
            tc[part(i), :] = beside(t_ref[part(i), :])

    def pair_square():
        a2a_wait(A2A_K, k_l)
        total = jnp.zeros((b, b), F32)
        for i in range(w):
            total = total + exact(k_l[i], t_l[i], nt=True)
        up[...] = total

    def pick_d(count):
        arrived(NODE_D, d_cand.at[pl.ds(0, count)])
        dd_row[...] = d_cand[mine, side_of]
        slab_start(AG_D, lambda j: dd_row, dd.at[rows, :])
        dd[rows, :] = dd_row[...]

    def gather_d():
        arrived(AG_D, dd.at[other_rows, :])

    def push_d():
        slab_start(RS_D, lambda j: dp.at[:, block(j), :], rs_d.at[s])
        rs_d[s] = dp[:, rows, :]

    def square_d():
        d = dd[...]
        dp[0] = sandwich(rtc, rc, d)
        dp[1] = sandwich(ltc, lc, d)
        push_d()

    def send_d():
        arrived(RS_D, rs_d.at[others])
        total = rs_d[0]
        for k in range(1, ns):
            total = total + rs_d[k]
        d_row[...] = total
        node_start(NODE_D, d_row, d_cand.at[n], c0, c1)

    def push_u():
        slab_start(RS_U, lambda j: up.at[block(j), :], rs_u.at[s])
        rs_u[s] = up[rows, :]

    def send_u():
        arrived(RS_U, rs_u.at[others])
        total = rs_u[0]
        for k in range(1, ns):
            total = total + rs_u[k]
        u_row[...] = total
        node_start(NODE_U, u_row, u_cand.at[n], p0, p1)

    def spread_u():
        slab_start(AG_U, lambda j: xy_row, xy.at[:, rows, :])
        xy[:, rows, :] = xy_row[...]

    def pick_u(count):
        arrived(NODE_U, u_cand.at[pl.ds(0, count)])
        xy_row[0] = u_cand[left_child]
        xy_row[1] = u_cand[right_child]
        spread_u()

    def push_merged():
        slot = jnp.where(n == 3, 1, 0)

        def go(k, c):
            j = lax.rem(s + k + ns // 2, ns)
            remote(MERGE, up.at[block(j), :], m_u.at[slot, s], n // 2, j, MERGE + slot).start()
            return c

        lax.fori_loop(0, ns, go, 0)

    def pick_merged(slot):
        arrived(MERGE + slot, m_u.at[slot])
        total = m_u[slot, 0]
        for k in range(1, ns):
            total = total + m_u[slot, k]
        xy_row[slot] = total

    def gather_u():
        arrived(AG_U, xy.at[:, other_rows, :])

    def square_u():
        up[...] = up[...] + (sandwich(rc, rtc, xy[0]) + sandwich(lc, ltc, xy[1], add=k_l))

    def move_left():
        x = above(xy[0])
        for i in range(w):
            spread(s_x, i, product(x, tc[part(i), :]))
        a2a_start(A2A_X, s_x, x_l)

    def push_energy(square):
        terms = dd[...] * square
        total = terms[0:w, :]
        for k in range(1, ns):
            total = total + terms[k * w : (k + 1) * w, :]
        rs_e[s] = total
        slab_start(SLAB_E, lambda j: rs_e.at[s], rs_e.at[s])

    def own_energy():
        arrived(SLAB_E, rs_e.at[others])
        total = rs_e[0]
        for k in range(1, ns):
            total = total + rs_e[k]
        return total

    def wait_total():
        arrived(NODE_F, e_all)

    def drain_first():
        a2a_drain(A2A_L, s_l)
        a2a_drain(A2A_K, s_k)

        @pl.when(n < 8)
        def _():
            a2a_drain(A2A_R, s_r)

    factor = b**0.75

    @pl.when(leaf)
    def _():
        a2a_wait(A2A_L, t_l)
        pair_square()
        push_u()
        send_u()
        drain_first()
        pick_d(4)
        gather_d()

    @pl.when((n >= 4) & (n < 8))
    def _():
        right_forms()
        left_forms()
        pair_square()
        own_forms()
        pick_u(8)
        gather_u()
        square_u()
        push_u()
        send_u()
        move_left()
        drain_first()
        pick_d(2)
        gather_d()
        square_d()
        send_d()
        wait_total()
        node_start(NODE_F, e_all, e_all, 2 * n, 2 * n + 2)

    @pl.when((n == 2) | (n == 3))
    def _():
        right_forms()
        left_forms()
        pair_square()
        own_forms()
        drain_first()
        pick_d(1)
        gather_d()
        square_d()
        pick_u(4)
        send_d()
        gather_u()
        square_u()
        push_merged()
        push_energy(up[...])
        move_left()
        e_row[...] = own_energy()
        e_cand[n] = e_row[...]
        node_start(NODE_E, e_row, e_cand.at[n], 5 - n, 6 - n)
        arrived(NODE_E, e_cand.at[pl.ds(0, 2)])
        e_all[...] = e_cand[1] + (e_cand[2] + e_cand[3])

        @pl.when(n == 2)
        def _():
            node_start(NODE_F, e_all, e_all, 4, 8)
            node_start(NODE_F, e_all, e_all, 1, 2)

    @pl.when(n == 1)
    def _():
        right_forms()
        left_forms()
        pick_d(1)
        gather_d()
        d = dd[...]
        dp[0] = exact_sandwich(rt, d)
        dp[1] = exact_sandwich(lt, d)
        push_d()
        send_d()
        pair_square()
        push_energy(up[...])
        own_forms()
        own = own_energy()
        arrived(NODE_E, e_cand.at[0])
        e_row[...] = own + e_cand[0]
        node_start(NODE_E, e_row, e_cand.at[n], 2, 4)
        drain_first()
        pick_merged(0)
        pick_merged(1)
        spread_u()
        gather_u()
        square_u()
        push_merged()
        move_left()
        wait_total()
        node_start(NODE_F, e_all, e_all, 0, 1)

    @pl.when(n == 0)
    def _():
        chips = ns // 2
        chip, core = s // 2, lax.rem(s, 2)
        near = [chip, lax.rem(chip + 2, chips), lax.rem(chip + chips - 2, chips)]
        z_peer = s + 2 - 4 * lax.rem(chip, 2)
        holders = [s, z_peer, lax.rem(s + chips, ns), lax.rem(z_peer + chips, ns)]
        kept = len(holders)

        dd[...] = env_ref[...]
        right_forms()
        dp[0] = exact_sandwich(rt, env_ref[...])
        dp[1] = jnp.zeros((b, b), F32)
        push_d()
        send_d()
        left_forms()
        d = above(env_ref[...] * factor)
        for i in range(w):
            x_l[i] = product(d, lc[part(i), :])
        slab_start(A2A_Z, lambda j: x_l.at[:, block(j), :], z.at[0, rows])
        z[0, rows] = x_l[:, rows, :]
        pair_square()
        push_energy(up[...] + sandwich(lc, ltc, op_q))
        e_row[...] = own_energy()
        node_start(NODE_E, e_row, e_cand.at[n], 1, 2)
        arrived(A2A_Z, z.at[0, other_rows])
        for k in range(1, kept):
            remote(COPIES, z.at[0], z.at[k], n, holders[k]).start()
        q_side = beside(op_q)
        q_weights = jnp.concatenate([q_side, q_side], axis=0)
        same = lax.broadcasted_iota(jnp.int32, (b, b), 0) == lax.broadcasted_iota(jnp.int32, (b, b), 1)
        p_one[...] = op_p + jnp.where(same, 1.0, 0.0)

        def chip_rows(m):
            return pl.ds(pl.multiple_of(m * (2 * w), 2 * w), 2 * w)

        p_near = above(jnp.concatenate([p_one[chip_rows(m), :] for m in near], axis=0))
        drain_first()
        drained(A2A_Z, x_l.at[:, other_rows, :])
        drained(RS_D, dp.at[:, other_rows, :])
        drained(NODE_D, d_row)
        drained(SLAB_E, rs_e.at[others])
        drained(NODE_E, e_row)
        arrived(COPIES, z.at[pl.ds(1, kept - 1)])
        drained(COPIES, z.at[pl.ds(1, kept - 1)])

        def known(q, c):
            side = beside(z.reshape(kept * b * w, b)[pl.ds((q // w) * (b * w) + lax.rem(q, w), b, stride=w), :])
            zc[q] = side
            moved = dot(side, q_weights)
            base[q] = product(p_near, beside(moved[:, :b] + moved[:, b:]))
            return c

        lax.fori_loop(0, kept * w, known, 0)

        pick_merged(0)
        mine_at = pl.ds(pl.multiple_of(core * w, w), w)
        ahead_at = pl.ds(pl.multiple_of((core + 4) * w, w), w)
        behind_at = pl.ds(pl.multiple_of((core + 2) * w, w), w)
        for c in range(2):
            remote(AG_U, xy_row.at[0], x_near.at[ahead_at, :], n, 2 * near[1] + c).start()
            remote(AG_U, xy_row.at[0], x_near.at[behind_at, :], n, 2 * near[2] + c).start()
        remote(AG_U, xy_row.at[0], x_near.at[mine_at, :], n, s + 1 - 2 * core).start()
        x_near[mine_at, :] = xy_row[0]
        arrived(AG_U, x_near.at[pl.ds(0, 5 * w), :])
        x = above(x_near[...])
        x_own = above(x_near[0 : 2 * w, :])

        def span(m):
            return pl.ds(pl.multiple_of(m * w, w), w)

        for k in range(kept):
            count = 6 if k < 2 else 2
            for i in range(w):
                q = k * w + i
                g = product(x if k < 2 else x_own, zc[q]) + base[q, 0 : count * w, :]
                for t in range(count):
                    gb[t, q] = g[t * w : (t + 1) * w, :]
            for t in range(2, count):
                remote(A2A_X, gb.at[t, pl.ds(k * w, w)], out_ref.at[span(holders[k])], n, 2 * near[t // 2] + t % 2).start()
        for k in range(kept):
            remote(A2A_X, gb.at[1 - core, pl.ds(k * w, w)], out_ref.at[span(holders[k])], n, s + 1 - 2 * core).start()
            out_ref[span(holders[k])] = gb[core, pl.ds(k * w, w)]
        wait_total()
        drained(AG_U, x_near.at[pl.ds(0, 5 * w), :])
        arrived(A2A_X, out_ref.at[pl.ds(0, 12 * w)])
        drained(A2A_X, out_ref.at[pl.ds(0, 12 * w)])

    @pl.when(n >= 1)
    def _():
        @pl.when(n < 8)
        def _():
            a2a_wait(A2A_X, x_l)

        d = above(dd[...] * factor)
        for i in range(w):
            side = beside(k_l[i] + jnp.where(n < 8, x_l[i], 0.0))
            out_ref.reshape(b * w, b)[pl.ds(i, b, stride=w), :] = product(d, side)

    @pl.when(leaf)
    def _():
        wait_total()

    en_ref[...] = jnp.sum(e_all[...], axis=(0, 1), keepdims=True)

    @pl.when((n >= 1) & (n < 8))
    def _():
        a2a_drain(A2A_X, s_x)
        drained(RS_D, dp.at[:, other_rows, :])
        drained(AG_U, xy.at[:, other_rows, :])

    @pl.when(n >= 1)
    def _():
        drained(AG_D, dd.at[other_rows, :])

    @pl.when(n >= 4)
    def _():
        drained(RS_U, up.at[other_rows, :])

    @pl.when((n >= 1) & (n < 4))
    def _():
        drained(MERGE, up)
        drained(SLAB_E, rs_e.at[others])

    @pl.when(n == 1)
    def _():
        drained(NODE_D, d_cand.at[pl.ds(0, 2)])
        drained(NODE_E, e_cand.at[pl.ds(0, 2)])
        drained(NODE_F, e_all)

    @pl.when((n == 2) | (n == 3))
    def _():
        drained(NODE_D, d_cand.at[pl.ds(0, 4)])
        drained(NODE_E, e_row)

    @pl.when(n == 2)
    def _():
        drained(NODE_F, e_cand.at[pl.ds(0, 5)])

    @pl.when((n >= 4) & (n < 8))
    def _():
        drained(NODE_D, d_cand.at[pl.ds(0, 8)])
        drained(NODE_U, u_cand.at[pl.ds(0, 2)])
        drained(NODE_F, e_cand.at[pl.ds(0, 2)])

    @pl.when(leaf)
    def _():
        drained(NODE_U, u_cand.at[pl.ds(0, 4)])


def per_device(ns, tensors, ops, assign, parent, env):
    b = env.shape[0]
    w = b // ns
    stack = pltpu.VMEM((w * b, b), F32)
    full = pltpu.VMEM((b, w, b), F32)
    form = pltpu.VMEM((w, b, b), F32)
    cat = pltpu.VMEM((w * b, 2 * b), BF16)
    square = pltpu.VMEM((b, b), F32)
    slab = pltpu.VMEM((w, b), F32)
    two = pltpu.VMEM((2, w, b), F32)
    hbm = pl.BlockSpec(memory_space=pl.ANY)
    vmem = pl.BlockSpec(memory_space=pltpu.VMEM)
    grad, energy = pl.pallas_call(
        functools.partial(kernel, ns),
        out_shape=(pltpu.VMEM((b, w, b), F32), jax.ShapeDtypeStruct((1, 1), F32)),
        in_specs=[hbm] * 5,
        out_specs=(vmem, vmem),
        scratch_shapes=[
            stack, pltpu.VMEM(ops.shape, F32), square,
            pltpu.SMEM((2, NODES), jnp.int32), pltpu.SMEM((NODES,), jnp.int32), pltpu.SemaphoreType.DMA((5,)),
            full, full, full, full, form, form, form, form, form, form,
            cat, cat, cat, cat, cat, pltpu.VMEM((2, ns, w, b), F32),
            square, pltpu.VMEM((ns, w, b), F32), slab, pltpu.VMEM((NODES, w, b), F32), two, pltpu.VMEM((2, b, b), F32),
            pltpu.VMEM((2, b, b), F32), pltpu.VMEM((ns, 2, w, b), F32), two,
            pltpu.VMEM((NODES, 2, w, b), F32), slab, square,
            pltpu.VMEM((ns, w, b), F32), slab, pltpu.VMEM((NODES, w, b), F32), slab,
            pltpu.VMEM((4, b, w, b), F32), pltpu.VMEM((4 * w, b, 2 * b), BF16), pltpu.VMEM((4 * w, 6 * w, b), F32),
            pltpu.VMEM((6, 4 * w, w, b), F32), pltpu.VMEM((6 * w, b), F32), square,
            pltpu.SemaphoreType.DMA((COUNT,)), pltpu.SemaphoreType.DMA((COUNT,)),
        ],
        compiler_params=pltpu.CompilerParams(collective_id=0, has_side_effects=True),
    )(tensors.reshape(w * b, b), ops, env, assign.T, parent)
    return grad[None], energy[0, 0]


def solution(mesh):
    return jax.shard_map(
        functools.partial(per_device, mesh.shape["slab"]),
        mesh=mesh,
        in_specs=(P("node", "slab", None, None), P(), P(), P(), P()),
        out_specs=(P("node", None, "slab", None), P()),
        check_vma=False,
    )
```

time: 95.5 us -> 87 us (0.911)
  Pallas kernels: 92.2 us -> 83.7 us
    pallas_call x1, Pallas kernels: 92.2 us -> 83.7 us  [per_device(): pl.pallas_call(functools.partial(kernel, ns), out_shape=(pltpu.VMEM((b, w...]
where the time goes in v4:
time: 87 us; the launch traced here: 86.8 us
  Pallas kernels  83.7 us (96%)
  between operations  2.33 us (3%)
    pallas_call x1, Pallas kernels, per_device(): pl.pallas_call(functools.partial(kernel, ns), out_shape=(pltpu.VMEM((b, w...  83.7 us

profile of v4, /device:TPU:1, one launch (start us, length us, event | category | flops | bytes accessed | tf_op | source)
XLA Modules:
  0.0 86.8 jit_solution(9449547158506745859)
XLA Ops:
  0.6 83.7 %shard_map.68 = (f32[128,8,128]{2,1,0:T(8,128)S(1)}, f32[1,1]{1,0:T(1,128)}) custom-call(f32[1024,128]{1,0:T(8,128)} %bitcast.5, f32[8,128,128]{2,1,0:T(8,128)} %ops_hbm.1, f32[128,128]{1,0:T(8,128)} %env_hbm.1, s32[2,16]{1,0:T(2,128)} %bitcast.6, s32[16]{0:T(128)} %parent_hbm.1), custom_call_target="tpu_custom_call" | custom-call | tf_op jit(solution)/shard_map/pallas_call | solution.py:614
  84.4 0.8 copy.9

commit v5 on v4

--- a/solution.py
+++ b/solution.py
@@ -95,7 +95,12 @@
 
     @pl.when(n >= 2)
     def _():
-        lax.fori_loop(c0, c1, greet_node, 0)
+        def greet_child(m, c):
+            to = jnp.where(m >= 12, s + 2 - 4 * lax.rem(s // 2, 2), s)
+            pl.semaphore_signal(barrier, inc=1, device_id=(m, to), device_id_type=MESH)
+            return c
+
+        lax.fori_loop(c0, c1, greet_child, 0)
 
     @pl.when(n < 2)
     def _():
@@ -112,6 +117,9 @@
 
     pair_of_two = jnp.where((n == 2) | (n == 3), 1, 0)
     greetings = (ns - 1) + jnp.where((n >= 1) & (n < 4), ns, p1 - p0) + (c1 - c0) + pair_of_two
+
+    def owned(m, j):
+        return jnp.where(m >= 12, j + 2 - 4 * lax.rem(j // 2, 2), j)
 
     def peer(k):
         return lax.rem(s + 1 + lax.rem(k + ns // 2 - 2, ns - 1), ns)
@@ -136,9 +144,9 @@
 
         lax.fori_loop(1, ns, go, 0)
 
-    def node_start(q, src, dst, lo, hi):
+    def node_start(q, src, dst, lo, hi, slab=s):
         def go(m, c):
-            remote(q, src, dst, m, s).start()
+            remote(q, src, dst, m, slab).start()
             return c
 
         lax.fori_loop(lo, hi, go, 0)
@@ -284,8 +292,8 @@
         node_start(NODE_D, d_row, d_cand.at[n], c0, c1)
 
     def push_u():
-        slab_start(RS_U, lambda j: up.at[block(j), :], rs_u.at[s])
-        rs_u[s] = up[rows, :]
+        slab_start(RS_U, lambda j: up.at[block(owned(n, j)), :], rs_u.at[s])
+        rs_u[s] = up[block(owned(n, s)), :]
 
     def send_u():
         arrived(RS_U, rs_u.at[others])
@@ -293,7 +301,7 @@
         for k in range(1, ns):
             total = total + rs_u[k]
         u_row[...] = total
-        node_start(NODE_U, u_row, u_cand.at[n], p0, p1)
+        node_start(NODE_U, u_row, u_cand.at[n], p0, p1, owned(n, s))
 
     def spread_u():
         slab_start(AG_U, lambda j: xy_row, xy.at[:, rows, :])
@@ -613,7 +621,7 @@
     vmem = pl.BlockSpec(memory_space=pltpu.VMEM)
     grad, energy = pl.pallas_call(
         functools.partial(kernel, ns),
-        out_shape=(pltpu.VMEM((b, w, b), F32), jax.ShapeDtypeStruct((1, 1), F32)),
+        out_shape=(pltpu.VMEM((b, w, b), F32), pltpu.VMEM((1, 1), F32)),
         in_specs=[hbm] * 5,
         out_specs=(vmem, vmem),
         scratch_shapes=[

time: 87 us -> 85.9 us (0.987)
  no operation moved by 1% of the time
where the time goes in v5:
time: 85.9 us; the launch traced here: 85.8 us
  Pallas kernels  83.2 us (97%)
  between operations  1.8 us (2%)
    pallas_call x1, Pallas kernels, per_device(): pl.pallas_call(functools.partial(kernel, ns), out_shape=(pltpu.VMEM((b, w...  83.2 us

profile of v5, /device:TPU:1, one launch (start us, length us, event | category | flops | bytes accessed | tf_op | source)
XLA Modules:
  0.0 85.8 jit_solution(4731277175289185123)
XLA Ops:
  0.6 83.2 %shard_map.68 = (f32[128,8,128]{2,1,0:T(8,128)S(1)}, f32[1,1]{1,0:T(1,128)S(1)}) custom-call(f32[1024,128]{1,0:T(8,128)} %bitcast.5, f32[8,128,128]{2,1,0:T(8,128)} %ops_hbm.1, f32[128,128]{1,0:T(8,128)} %env_hbm.1, s32[2,16]{1,0:T(2,128)} %bitcast.6, s32[16]{0:T(128)} %parent_hbm.1), custom_call_target="tpu_custom_call" | custom-call | tf_op jit(solution)/shard_map/pallas_call | solution.py:622
  83.8 0.8 copy.9

commit v6 on v5

--- a/solution.py
+++ b/solution.py
@@ -409,12 +409,12 @@
         drain_first()
         pick_d(1)
         gather_d()
+        pick_u(4)
         square_d()
-        pick_u(4)
-        send_d()
         gather_u()
         square_u()
         push_merged()
+        send_d()
         push_energy(up[...])
         move_left()
         e_row[...] = own_energy()
@@ -500,8 +500,6 @@
         drained(NODE_D, d_row)
         drained(SLAB_E, rs_e.at[others])
         drained(NODE_E, e_row)
-        arrived(COPIES, z.at[pl.ds(1, kept - 1)])
-        drained(COPIES, z.at[pl.ds(1, kept - 1)])
 
         def known(q, c):
             side = beside(z.reshape(kept * b * w, b)[pl.ds((q // w) * (b * w) + lax.rem(q, w), b, stride=w), :])
@@ -510,7 +508,10 @@
             base[q] = product(p_near, beside(moved[:, :b] + moved[:, b:]))
             return c
 
-        lax.fori_loop(0, kept * w, known, 0)
+        lax.fori_loop(0, w, known, 0)
+        arrived(COPIES, z.at[pl.ds(1, kept - 1)])
+        drained(COPIES, z.at[pl.ds(1, kept - 1)])
+        lax.fori_loop(w, kept * w, known, 0)
 
         pick_merged(0)
         mine_at = pl.ds(pl.multiple_of(core * w, w), w)

time: 85.9 us -> 82.3 us (0.958)
  Pallas kernels: 83.2 us -> 79.6 us
    pallas_call x1, Pallas kernels: 83.2 us -> 79.6 us  [per_device(): pl.pallas_call(functools.partial(kernel, ns), out_shape=(pltpu.VMEM((b, w...]
where the time goes in v6:
time: 82.3 us; the launch traced here: 82.2 us
  Pallas kernels  79.6 us (97%)
  between operations  1.8 us (2%)
    pallas_call x1, Pallas kernels, per_device(): pl.pallas_call(functools.partial(kernel, ns), out_shape=(pltpu.VMEM((b, w...  79.6 us

profile of v6, /device:TPU:1, one launch (start us, length us, event | category | flops | bytes accessed | tf_op | source)
XLA Modules:
  0.0 82.2 jit_solution(15340669475243151941)
XLA Ops:
  0.6 79.6 %shard_map.68 = (f32[128,8,128]{2,1,0:T(8,128)S(1)}, f32[1,1]{1,0:T(1,128)S(1)}) custom-call(f32[1024,128]{1,0:T(8,128)} %bitcast.5, f32[8,128,128]{2,1,0:T(8,128)} %ops_hbm.1, f32[128,128]{1,0:T(8,128)} %env_hbm.1, s32[2,16]{1,0:T(2,128)} %bitcast.6, s32[16]{0:T(128)} %parent_hbm.1), custom_call_target="tpu_custom_call" | custom-call | tf_op jit(solution)/shard_map/pallas_call | solution.py:623
  80.3 0.8 copy.9

commit v7 on v6

--- a/solution.py
+++ b/solution.py
@@ -69,7 +69,7 @@
         pltpu.make_async_copy(assign_hbm, assign_ref, in_sem.at[3]),
         pltpu.make_async_copy(parent_hbm, parent_ref, in_sem.at[4]),
     ]
-    for load in (loads[0], loads[3], loads[4]):
+    for load in loads:
         load.start()
 
     def block(j):
@@ -201,8 +201,6 @@
         return first, last
 
     loads[0].wait()
-    loads[1].start()
-    loads[2].start()
 
     @pl.when(n < 8)
     def _():
@@ -483,7 +481,7 @@
         e_row[...] = own_energy()
         node_start(NODE_E, e_row, e_cand.at[n], 1, 2)
         arrived(A2A_Z, z.at[0, other_rows])
-        for k in range(1, kept):
+        for k in (3, 2, 1):
             remote(COPIES, z.at[0], z.at[k], n, holders[k]).start()
         q_side = beside(op_q)
         q_weights = jnp.concatenate([q_side, q_side], axis=0)

time: 82.3 us -> 82 us (level)
  no operation moved by 1% of the time
where the time goes in v7:
time: 82 us; the launch traced here: 81.9 us
  Pallas kernels  79.3 us (97%)
  between operations  1.8 us (2%)
    pallas_call x1, Pallas kernels, per_device(): pl.pallas_call(functools.partial(kernel, ns), out_shape=(pltpu.VMEM((b, w...  79.3 us

profile of v7, /device:TPU:1, one launch (start us, length us, event | category | flops | bytes accessed | tf_op | source)
XLA Modules:
  0.0 81.9 jit_solution(17545811642871443210)
XLA Ops:
  0.6 79.3 %shard_map.68 = (f32[128,8,128]{2,1,0:T(8,128)S(1)}, f32[1,1]{1,0:T(1,128)S(1)}) custom-call(f32[1024,128]{1,0:T(8,128)} %bitcast.5, f32[8,128,128]{2,1,0:T(8,128)} %ops_hbm.1, f32[128,128]{1,0:T(8,128)} %env_hbm.1, s32[2,16]{1,0:T(2,128)} %bitcast.6, s32[16]{0:T(128)} %parent_hbm.1), custom_call_target="tpu_custom_call" | custom-call | tf_op jit(solution)/shard_map/pallas_call | solution.py:621
  80.0 0.8 copy.9
